TPU v7x, 32 devices: a whole 2x2x4 slice. The times are simulated.
32 devices in a mesh: src: 4 (over x, core), dst: 2 (over y), tm: 4 (over z).
Axes of the slice: x: 2, y: 2, z: 4, core: 2. Of those that a mesh axis runs over, the one named last changes fastest.
Arguments:
- traffic: bfloat16 [256, 256, 512], P('src', 'dst', 'tm'), may hold values from -6 to 6
- src_factor: float32 [256, 64], P('src'), may hold values from -0.75 to 0.75
- dst_factor: float32 [256, 64], P('dst'), may hold values from -0.75 to 0.75
- time_factor: float32 [512, 64], P('tm'), may hold values from -0.75 to 0.75
Outputs:
- grad_src: float32 [256, 64], P('src')
- grad_dst: float32 [256, 64], P('dst')
- grad_time: float32 [512, 64], P('tm')
All inputs are finite; a program needn't handle non-finite values.
Results may differ from a plain program's by a relative error of at most 0.0003.
Values sent between devices are 32-bit elements; how exact they have to be, the bound alone decides.
No kernel may reach another device: no remote copies, remote signals or barrier semaphores. Data moves between devices by JAX's collectives and lax.ppermute only.
A program may use at most 64 MiB of HBM per device.

v0:
```python
import functools

import jax
import jax.numpy as jnp
from jax import lax
from jax.experimental import pallas as pl
from jax.experimental.pallas import tpu as pltpu
from jax.sharding import PartitionSpec as P


DAY = 288
STEPS = 3

hour_weight = 32.0
day_weight = 64.0
step_rate = 0.1
highest = lax.Precision.HIGHEST
f32 = jnp.float32
bf16 = jnp.bfloat16
LANES = 128
AXES = ("src", "dst", "tm")
BY_LANES = (((1,), (1,)), ((), ()))
VMEM = pl.BlockSpec(memory_space=pltpu.VMEM)
PARAMS = pltpu.CompilerParams(vmem_limit_bytes=24 << 20)


def halves(x):
    high = x.astype(bf16)
    low = (x - high.astype(f32)).astype(bf16)
    return jnp.concatenate([high, low], 0)


def gram(x):
    return lax.dot_general(x, x, BY_LANES, precision=highest, preferred_element_type=f32)


def times(a, b):
    return jnp.dot(a, b, precision=highest, preferred_element_type=f32)


def packed(x):
    fold = LANES // x.shape[1] if x.shape[1] < LANES else 1
    rows = x.shape[0] // fold
    return x if fold == 1 else jnp.concatenate([x[i * rows : (i + 1) * rows] for i in range(fold)], 1)


def unpacked(x, columns):
    fold = x.shape[1] // columns
    return x if fold == 1 else jnp.concatenate([x[:, i * columns : (i + 1) * columns] for i in range(fold)], 0)


def place_of(count):
    place = lax.axis_index("src") * (lax.axis_size("dst") // 2) + lax.axis_index("dst") // 2
    return jnp.minimum(place, count - 1), place < count


def src_dst_part(slice_rows, traffic, src_now, dst_now, time_now, time, out, ready=None):
    rank = src_now.shape[1]
    src_rows, dst_rows, time_rows = traffic.shape
    time_halves = halves(time_now)
    dst_wide = jnp.concatenate([dst_now, dst_now], 0).T
    src_wide = jnp.concatenate([src_now, src_now], 1)
    dst_sum = jnp.zeros((dst_rows, 2 * rank), f32)
    rows = []
    step = 4
    for first in range(0, src_rows, step):
        if ready is not None:
            ready(first)
        block = traffic[first : first + step].reshape(step * dst_rows, time_rows)
        seen = lax.dot_general(block, time_halves, BY_LANES, preferred_element_type=f32)
        for i in range(step):
            part = seen[i * dst_rows : (i + 1) * dst_rows]
            dst_sum = dst_sum + part * src_wide[first + i : first + i + 1]
            rows.append(jnp.sum(part * dst_wide, axis=0, keepdims=True))
    src_sum = jnp.concatenate(rows, 0)
    dst_seen = (dst_sum[:, :rank] + dst_sum[:, rank:]).T
    time_gram = gram(time_now)
    src_part = times(src_now, gram(dst_now) * time_gram) - (src_sum[:, :rank] + src_sum[:, rank:])
    dst_part = times(gram(src_now.T) * time_gram, dst_now) - dst_seen
    src_packed = packed(src_part)
    top = src_packed.shape[0]
    out[:top] = src_packed
    out[top : top + rank] = dst_part
    start = pl.multiple_of(place_of(rank // slice_rows)[0] * slice_rows, slice_rows)
    out[top + rank :] = time[pl.ds(start, slice_rows)]


def src_dst_kernel(slice_rows, traffic, src, dst, time, out):
    src_dst_part(slice_rows, traffic, src[...], dst[...], time[...], time, out)


def entry_kernel(slice_rows, traffic_in, src_in, dst_in, time_in, out, traffic, src, dst, time, arrived):
    chunks = arrived.shape[0] - 3
    chunk = traffic.shape[0] // chunks
    small = [
        pltpu.make_async_copy(a, b, arrived.at[chunks + i])
        for i, (a, b) in enumerate(((src_in, src), (dst_in, dst), (time_in, time)))
    ]
    large = [
        pltpu.make_async_copy(
            traffic_in.at[pl.ds(i * chunk, chunk)], traffic.at[pl.ds(i * chunk, chunk)], arrived.at[i]
        )
        for i in range(chunks)
    ]
    for copy in small + large:
        copy.start()
    for copy in small:
        copy.wait()

    def ready(first):
        if first % chunk == 0:
            large[first // chunk].wait()

    src_dst_part(slice_rows, traffic, src[...], dst[...], time[...], time, out, ready)


def time_kernel(traffic, src, dst, time, out):
    src_now, dst_now, time_now = src[...].T, dst[...], time[...]
    rank, src_rows = src_now.shape
    dst_halves = halves(dst_now)
    total = times(gram(src_now) * gram(dst_now), time_now)
    seen_sum = jnp.zeros(total.shape, f32)
    for i in range(src_rows):
        seen = jnp.dot(dst_halves, traffic[i], preferred_element_type=f32)
        seen_sum = seen_sum + (seen[:rank] + seen[rank:]) * src_now[:, i : i + 1]
    out[...] = total - seen_sum


def back(x, offset, position):
    if offset >= x.shape[1]:
        return jnp.zeros_like(x)
    return jnp.where(position >= offset, pltpu.roll(x, offset, 1), 0.0)


def forth(x, offset, position):
    size = x.shape[1]
    if offset >= size:
        return jnp.zeros_like(x)
    return jnp.where(position < size - offset, pltpu.roll(x, size - offset, 1), 0.0)


def smooth_kernel(slice_rows, src_top, blocks, *refs):
    held, time_part, src_time_out, dst_time_out = refs[:blocks], refs[blocks], refs[-2], refs[-1]
    rank, time_rows = time_part.shape
    here = lax.axis_index("tm")
    total = held[0][: src_top + rank]
    for other in held[1:]:
        total = total + other[: src_top + rank]
    src_time_out[:src_top] = total[:src_top]
    src_time_out[src_top:] = time_part[...]
    dst_time_out[:rank] = total[src_top:]
    slices = [h[src_top + rank :] for h in held]
    ordered = []
    for block in range(blocks):
        pick = slices[0]
        for mask in range(1, blocks):
            pick = jnp.where((here ^ block) == mask, slices[mask], pick)
        ordered.append(pick)
    whole = jnp.concatenate(ordered, 1)
    position = lax.broadcasted_iota(jnp.int32, whole.shape, 1)
    hour_diff = jnp.where(position >= 1, whole - back(whole, 1, position), 0.0)
    day_diff = jnp.where(position >= DAY, whole - back(whole, DAY, position), 0.0)
    smooth = hour_weight * (hour_diff - forth(hour_diff, 1, position))
    smooth = smooth + day_weight * (day_diff - forth(day_diff, DAY, position))
    mine = smooth[:, :time_rows]
    for block in range(1, blocks):
        mine = jnp.where(here == block, smooth[:, block * time_rows : (block + 1) * time_rows], mine)
    dst_time_out[rank:] = time_part[...]
    place, smooths = place_of(rank // slice_rows)
    mine = jnp.where(smooths, mine, 0.0)
    start = pl.multiple_of(rank + place * slice_rows, slice_rows)
    dst_time_out[pl.ds(start, slice_rows)] = dst_time_out[pl.ds(start, slice_rows)] + mine


def exchanged(x, src_mask, dst_mask, tm_mask):
    src_size, dst_size, tm_size = (lax.axis_size(a) for a in AXES)
    route = []
    for s in range(src_size):
        for d in range(dst_size):
            for t in range(tm_size):
                here = (s * dst_size + d) * tm_size + t
                there = ((s ^ src_mask) * dst_size + (d ^ dst_mask)) * tm_size + (t ^ tm_mask)
                route.append((here, there))
    return lax.ppermute(x, AXES, route)


def on_device(traffic, src_factor, dst_factor, time_factor):
    src_rows, rank = src_factor.shape
    src_size, dst_size, tm_size = (lax.axis_size(a) for a in AXES)
    slice_rows = max(8, rank // (src_size * dst_size // 2))
    dst_rows, time_rows = dst_factor.shape[0], time_factor.shape[0]
    src_top = rank * src_rows // LANES if src_rows < LANES else src_rows
    mixed_shape = jax.ShapeDtypeStruct((src_top + rank + slice_rows, LANES), f32)
    zero_kernel = pl.pallas_call(
        functools.partial(entry_kernel, slice_rows),
        out_shape=(
            mixed_shape,
            jax.ShapeDtypeStruct(traffic.shape, traffic.dtype),
            jax.ShapeDtypeStruct((src_rows, rank), f32),
            jax.ShapeDtypeStruct((rank, dst_rows), f32),
            jax.ShapeDtypeStruct((rank, time_rows), f32),
        ),
        in_specs=[pl.BlockSpec(memory_space=pltpu.HBM)] * 4,
        out_specs=(VMEM,) * 5,
        scratch_shapes=[pltpu.SemaphoreType.DMA((4 + 3,))],
        compiler_params=PARAMS,
        name="entry",
    )
    first_kernel = pl.pallas_call(
        functools.partial(src_dst_kernel, slice_rows),
        out_shape=mixed_shape,
        in_specs=[VMEM] * 4,
        out_specs=VMEM,
        compiler_params=PARAMS,
        name="src_dst_part",
    )
    second_kernel = pl.pallas_call(
        time_kernel,
        out_shape=jax.ShapeDtypeStruct((rank, time_rows), f32),
        in_specs=[VMEM] * 4,
        out_specs=VMEM,
        compiler_params=PARAMS,
        name="time_part",
    )
    third_kernel = pl.pallas_call(
        functools.partial(smooth_kernel, slice_rows, src_top, tm_size),
        out_shape=(
            jax.ShapeDtypeStruct((src_top + rank, LANES), f32),
            jax.ShapeDtypeStruct((2 * rank, LANES), f32),
        ),
        in_specs=[VMEM] * (tm_size + 1),
        out_specs=(VMEM, VMEM),
        compiler_params=PARAMS,
        name="tm_sums",
    )
    for iteration in range(STEPS):
        if iteration == 0:
            given = (traffic, src_factor, dst_factor.T, time_factor.T)
            given = [pltpu.with_memory_space_constraint(x, pltpu.HBM) for x in given]
            mixed, traffic, src_now, dst_now, time_now = zero_kernel(*given)
        else:
            mixed = first_kernel(traffic, src_now, dst_now, time_now)
        others = [exchanged(mixed, 0, 0, mask) for mask in range(1, tm_size)]
        time_part = second_kernel(traffic, src_now, dst_now, time_now)
        add_time = exchanged(time_part, 2, 1, 0)
        src_time, dst_time = third_kernel(mixed, *others, time_part)
        src_mask, dst_mask = 2, 1
        while src_mask < src_size or dst_mask < dst_size:
            if src_mask > 2:
                src_time = jnp.concatenate([src_sum, dst_time[rank:]], 0)
                both = src_mask < src_size and dst_mask < dst_size
                add_time = exchanged(dst_time[rank:], src_mask, dst_mask, 0) if both else 0.0
            src_sum = src_time[:src_top]
            add_dst = 0.0
            if src_mask < src_size:
                other = exchanged(dst_time, src_mask, 0, 0)
                add_dst, add_time = other[:rank], add_time + other[rank:]
            if dst_mask < dst_size:
                other = exchanged(src_time, 0, dst_mask, 0)
                src_sum, add_time = src_sum + other[:src_top], add_time + other[src_top:]
            dst_time = jnp.concatenate([dst_time[:rank] + add_dst, dst_time[rank:] + add_time], 0)
            src_mask, dst_mask = src_mask * 2, dst_mask * 2
        dst_time = dst_time + exchanged(dst_time, 1, 0, 0)
        grad_src = unpacked(src_sum, rank) / rank
        grad_dst = dst_time[:rank] / rank
        grad_time = dst_time[rank:] / rank
        if iteration + 1 < STEPS:
            src_now = src_now - step_rate * grad_src
            dst_now = dst_now - step_rate * grad_dst
            time_now = time_now - step_rate * grad_time
    return (grad_src, grad_dst.T, grad_time.T)


def solution(mesh):
    in_specs = (P("src", "dst", "tm"), P("src", None), P("dst", None), P("tm", None))
    out_specs = (P("src", None), P("dst", None), P("tm", None))
    return jax.shard_map(
        on_device, mesh=mesh, in_specs=in_specs, out_specs=out_specs, check_vma=False
    )
```

profile of v0, /device:TPU:0, one launch (start us, length us, event | category | flops | bytes accessed | tf_op | source)
XLA Modules:
  0.0 61.0 jit_solution(13679492214325754097)
XLA Ops:
  0.6 2.8 %entry.1 = (f32[112,128]{1,0:T(8,128)S(1)}, bf16[64,128,128]{2,1,0:T(8,128)(2,1)S(1)}, f32[64,64]{1,0:T(8,128)S(1)}, f32[64,128]{1,0:T(8,128)S(1)}, f32[64,128]{1,0:T(8,128)S(1)}) custom-call(bf16[64,128,128]{2,1,0:T(8,128)(2,1)} %traffic_in.1, f32[64,64]{1,0:T(8,128)} %src_in.1, f32[64,128]{1,0:T(8,128)} %bitcast.6, f32[64,128]{1,0:T(8,128)} %bitcast.7), custom_call_target="tpu_custom_call" | custom-call | tf_op jit(solution)/shard_map/entry/pallas_call | solution.py:240
  3.4 3.1 %collective-permute-start = (f32[112,128]{1,0:T(8,128)S(1)}, f32[112,128]{1,0:T(8,128)S(1)}, u32[]{:S(2)}, u32[]{:S(2)}) collective-permute-start(f32[112,128]{1,0:T(8,128)S(1)} %get-tuple-element.16.refs_0_), channel_id=1, source_target_pairs={{0,1},{1,0},{2,3},{3,2},{4,5},{5,4},{6,7},{7,6},{8,9},{9,8},{10,11... | collective-permute-start | bytes 172040 | tf_op jit(solution)/shard_map/ppermute | solution.py:184
  6.6 2.6 %collective-permute-start.1 = (f32[112,128]{1,0:T(8,128)S(1)}, f32[112,128]{1,0:T(8,128)S(1)}, u32[]{:S(2)}, u32[]{:S(2)}) collective-permute-start(f32[112,128]{1,0:T(8,128)S(1)} %get-tuple-element.16.refs_0_), channel_id=1, source_target_pairs={{0,2},{1,3},{2,0},{3,1},{4,6},{5,7},{6,4},{7,5},{8,10},{9,11},{10,... | collective-permute-start | bytes 172040 | tf_op jit(solution)/shard_map/ppermute | solution.py:184
  9.2 1.0 %time_part.3.refs_4_ = f32[64,128]{1,0:T(8,128)S(1)} custom-call(bf16[64,128,128]{2,1,0:T(8,128)(2,1)S(1)} %get-tuple-element.14.traffic, f32[64,64]{1,0:T(8,128)S(1)} %get-tuple-element.15.src, f32[64,128]{1,0:T(8,128)S(1)} %get-tuple-element.17.dst, f32[64,128]{1,0:T(8,128)S(1)} %get-tuple-element.18.time), custom_call_target="tpu_custom_call" | custom-call | tf_op jit(solution)/shard_map/time_part/pallas_call | solution.py:244
  10.2 2.6 %collective-permute-done.1.refs_2_ = f32[112,128]{1,0:T(8,128)S(1)} collective-permute-done((f32[112,128]{1,0:T(8,128)S(1)}, f32[112,128]{1,0:T(8,128)S(1)}, u32[]{:S(2)}, u32[]{:S(2)}) %collective-permute-start.1) | collective-permute-done | bytes 57376 | tf_op jit(solution)/shard_map/ppermute | solution.py:184
  12.8 2.4 %collective-permute-done.2.refs_3_ = f32[112,128]{1,0:T(8,128)S(1)} collective-permute-done((f32[112,128]{1,0:T(8,128)S(1)}, f32[112,128]{1,0:T(8,128)S(1)}, u32[]{:S(2)}, u32[]{:S(2)}) %collective-permute-start.2) | collective-permute-done | bytes 57376 | tf_op jit(solution)/shard_map/ppermute | solution.py:184
  15.1 0.2 tm_sums.3
  15.3 1.6 %collective-permute-start.3 = (f32[96,128]{1,0:T(8,128)S(1)}, f32[96,128]{1,0:T(8,128)S(1)}, u32[]{:S(2)}, u32[]{:S(2)}) collective-permute-start(f32[96,128]{1,0:T(8,128)S(1)} %get-tuple-element.19), channel_id=1, source_target_pairs={{0,4},{1,5},{2,6},{3,7},{4,0},{5,1},{6,2},{7,3},{8,12},{9,13},{10,... | collective-permute-start | bytes 147464 | tf_op jit(solution)/shard_map/ppermute | solution.py:184
  16.9 1.5 %collective-permute-start.5 = (f32[64,128]{1,0:T(8,128)S(1)}, f32[64,128]{1,0:T(8,128)S(1)}, u32[]{:S(2)}, u32[]{:S(2)}) collective-permute-start(f32[64,128]{1,0:T(8,128)S(1)} %time_part.3.refs_4_), channel_id=1, source_target_pairs={{0,20},{1,21},{2,22},{3,23},{4,16},{5,17},{6,18},{7,19},{8,28},{9,... | collective-permute-start | bytes 98312 | tf_op jit(solution)/shard_map/ppermute | solution.py:184
  18.4 0.5 collective-permute-start.4
  18.9 0.6 collective-permute-done.3
  19.5 0.1 fusion.16
  19.5 2.2 %collective-permute-done.5 = f32[64,128]{1,0:T(8,128)S(1)} collective-permute-done((f32[64,128]{1,0:T(8,128)S(1)}, f32[64,128]{1,0:T(8,128)S(1)}, u32[]{:S(2)}, u32[]{:S(2)}) %collective-permute-start.5) | collective-permute-done | bytes 32800 | tf_op jit(solution)/shard_map/ppermute | solution.py:184
  21.7 0.9 %collective-permute-done.4 = f32[128,128]{1,0:T(8,128)S(1)} collective-permute-done((f32[128,128]{1,0:T(8,128)S(1)}, f32[128,128]{1,0:T(8,128)S(1)}, u32[]{:S(2)}, u32[]{:S(2)}) %collective-permute-start.4) | collective-permute-done | bytes 65568 | tf_op jit(solution)/shard_map/ppermute | solution.py:184
  22.7 1.2 %collective-permute-done.6 = f32[128,128]{1,0:T(8,128)S(1)} collective-permute-done((f32[128,128]{1,0:T(8,128)S(1)}, f32[128,128]{1,0:T(8,128)S(1)}, u32[]{:S(2)}, u32[]{:S(2)}) %collective-permute-start.6) | collective-permute-done | bytes 65568 | tf_op jit(solution)/shard_map/ppermute | solution.py:184
  24.0 1.2 %src_dst_part.2.refs_0_ = f32[112,128]{1,0:T(8,128)S(1)} custom-call(bf16[64,128,128]{2,1,0:T(8,128)(2,1)S(1)} %get-tuple-element.14.traffic, f32[64,64]{1,0:T(8,128)S(1)} %fusion.9.src, f32[64,128]{1,0:T(8,128)S(1)} %get-tuple-element.36.dst, f32[64,128]{1,0:T(8,128)S(1)} %get-tuple-element.35.time), custom_call_target="tpu_custom_call" | custom-call | tf_op jit(solution)/shard_map/src_dst_part/pallas_call | solution.py:242
  25.3 1.8 %collective-permute-start.8 = (f32[112,128]{1,0:T(8,128)S(1)}, f32[112,128]{1,0:T(8,128)S(1)}, u32[]{:S(2)}, u32[]{:S(2)}) collective-permute-start(f32[112,128]{1,0:T(8,128)S(1)} %src_dst_part.2.refs_0_), channel_id=1, source_target_pairs={{0,2},{1,3},{2,0},{3,1},{4,6},{5,7},{6,4},{7,5},{8,10},{9,11},{10,... | collective-permute-start | bytes 172040 | tf_op jit(solution)/shard_map/ppermute | solution.py:184
  27.1 2.6 %collective-permute-start.9 = (f32[112,128]{1,0:T(8,128)S(1)}, f32[112,128]{1,0:T(8,128)S(1)}, u32[]{:S(2)}, u32[]{:S(2)}) collective-permute-start(f32[112,128]{1,0:T(8,128)S(1)} %src_dst_part.2.refs_0_), channel_id=1, source_target_pairs={{0,3},{1,2},{2,1},{3,0},{4,7},{5,6},{6,5},{7,4},{8,11},{9,10},{10,... | collective-permute-start | bytes 172040 | tf_op jit(solution)/shard_map/ppermute | solution.py:184
  29.7 1.0 %time_part.4.refs_4_ = f32[64,128]{1,0:T(8,128)S(1)} custom-call(bf16[64,128,128]{2,1,0:T(8,128)(2,1)S(1)} %get-tuple-element.14.traffic, f32[64,64]{1,0:T(8,128)S(1)} %fusion.9.src, f32[64,128]{1,0:T(8,128)S(1)} %get-tuple-element.36.dst, f32[64,128]{1,0:T(8,128)S(1)} %get-tuple-element.35.time), custom_call_target="tpu_custom_call" | custom-call | tf_op jit(solution)/shard_map/time_part/pallas_call | solution.py:244
  30.7 2.7 %collective-permute-done.8.refs_2_ = f32[112,128]{1,0:T(8,128)S(1)} collective-permute-done((f32[112,128]{1,0:T(8,128)S(1)}, f32[112,128]{1,0:T(8,128)S(1)}, u32[]{:S(2)}, u32[]{:S(2)}) %collective-permute-start.8) | collective-permute-done | bytes 57376 | tf_op jit(solution)/shard_map/ppermute | solution.py:184
  33.4 0.2 tm_sums.4
  33.6 1.6 %collective-permute-start.10 = (f32[96,128]{1,0:T(8,128)S(1)}, f32[96,128]{1,0:T(8,128)S(1)}, u32[]{:S(2)}, u32[]{:S(2)}) collective-permute-start(f32[96,128]{1,0:T(8,128)S(1)} %get-tuple-element.21), channel_id=1, source_target_pairs={{0,4},{1,5},{2,6},{3,7},{4,0},{5,1},{6,2},{7,3},{8,12},{9,13},{10,... | collective-permute-start | bytes 147464 | tf_op jit(solution)/shard_map/ppermute | solution.py:184
  35.2 0.6 collective-permute-start.12
  35.7 1.4 %collective-permute-start.11 = (f32[128,128]{1,0:T(8,128)S(1)}, f32[128,128]{1,0:T(8,128)S(1)}, u32[]{:S(2)}, u32[]{:S(2)}) collective-permute-start(f32[128,128]{1,0:T(8,128)S(1)} %get-tuple-element.22), channel_id=1, source_target_pairs={{0,16},{1,17},{2,18},{3,19},{4,20},{5,21},{6,22},{7,23},{8,24},{9,... | collective-permute-start | bytes 196616 | tf_op jit(solution)/shard_map/ppermute | solution.py:184
  37.2 0.7 %collective-permute-done.10 = f32[96,128]{1,0:T(8,128)S(1)} collective-permute-done((f32[96,128]{1,0:T(8,128)S(1)}, f32[96,128]{1,0:T(8,128)S(1)}, u32[]{:S(2)}, u32[]{:S(2)}) %collective-permute-start.10) | collective-permute-done | bytes 49184 | tf_op jit(solution)/shard_map/ppermute | solution.py:184
  37.9 0.1 fusion.15
  38.0 2.0 %collective-permute-done.12 = f32[64,128]{1,0:T(8,128)S(1)} collective-permute-done((f32[64,128]{1,0:T(8,128)S(1)}, f32[64,128]{1,0:T(8,128)S(1)}, u32[]{:S(2)}, u32[]{:S(2)}) %collective-permute-start.12) | collective-permute-done | bytes 32800 | tf_op jit(solution)/shard_map/ppermute | solution.py:184
  40.0 0.1 collective-permute-start.13
  40.1 1.2 %collective-permute-done.13 = f32[128,128]{1,0:T(8,128)S(1)} collective-permute-done((f32[128,128]{1,0:T(8,128)S(1)}, f32[128,128]{1,0:T(8,128)S(1)}, u32[]{:S(2)}, u32[]{:S(2)}) %collective-permute-start.13) | collective-permute-done | bytes 65568 | tf_op jit(solution)/shard_map/ppermute | solution.py:184
  41.4 1.2 %src_dst_part.3.refs_0_ = f32[112,128]{1,0:T(8,128)S(1)} custom-call(bf16[64,128,128]{2,1,0:T(8,128)(2,1)S(1)} %get-tuple-element.14.traffic, f32[64,64]{1,0:T(8,128)S(1)} %fusion.10.src, f32[64,128]{1,0:T(8,128)S(1)} %get-tuple-element.34.dst, f32[64,128]{1,0:T(8,128)S(1)} %get-tuple-element.33.time), custom_call_target="tpu_custom_call" | custom-call | tf_op jit(solution)/shard_map/src_dst_part/pallas_call | solution.py:242
  42.6 1.3 %collective-permute-start.14 = (f32[112,128]{1,0:T(8,128)S(1)}, f32[112,128]{1,0:T(8,128)S(1)}, u32[]{:S(2)}, u32[]{:S(2)}) collective-permute-start(f32[112,128]{1,0:T(8,128)S(1)} %src_dst_part.3.refs_0_), channel_id=1, source_target_pairs={{0,1},{1,0},{2,3},{3,2},{4,5},{5,4},{6,7},{7,6},{8,9},{9,8},{10,11... | collective-permute-start | bytes 172040 | tf_op jit(solution)/shard_map/ppermute | solution.py:184
  43.9 1.6 %collective-permute-start.15 = (f32[112,128]{1,0:T(8,128)S(1)}, f32[112,128]{1,0:T(8,128)S(1)}, u32[]{:S(2)}, u32[]{:S(2)}) collective-permute-start(f32[112,128]{1,0:T(8,128)S(1)} %src_dst_part.3.refs_0_), channel_id=1, source_target_pairs={{0,2},{1,3},{2,0},{3,1},{4,6},{5,7},{6,4},{7,5},{8,10},{9,11},{10,... | collective-permute-start | bytes 172040 | tf_op jit(solution)/shard_map/ppermute | solution.py:184
  45.6 1.5 %collective-permute-start.16 = (f32[112,128]{1,0:T(8,128)S(1)}, f32[112,128]{1,0:T(8,128)S(1)}, u32[]{:S(2)}, u32[]{:S(2)}) collective-permute-start(f32[112,128]{1,0:T(8,128)S(1)} %src_dst_part.3.refs_0_), channel_id=1, source_target_pairs={{0,3},{1,2},{2,1},{3,0},{4,7},{5,6},{6,5},{7,4},{8,11},{9,10},{10,... | collective-permute-start | bytes 172040 | tf_op jit(solution)/shard_map/ppermute | solution.py:184
  47.1 1.0 %time_part.5.refs_4_ = f32[64,128]{1,0:T(8,128)S(1)} custom-call(bf16[64,128,128]{2,1,0:T(8,128)(2,1)S(1)} %get-tuple-element.14.traffic, f32[64,64]{1,0:T(8,128)S(1)} %fusion.10.src, f32[64,128]{1,0:T(8,128)S(1)} %get-tuple-element.34.dst, f32[64,128]{1,0:T(8,128)S(1)} %get-tuple-element.33.time), custom_call_target="tpu_custom_call" | custom-call | tf_op jit(solution)/shard_map/time_part/pallas_call | solution.py:244
  48.1 2.9 %collective-permute-done.15.refs_2_ = f32[112,128]{1,0:T(8,128)S(1)} collective-permute-done((f32[112,128]{1,0:T(8,128)S(1)}, f32[112,128]{1,0:T(8,128)S(1)}, u32[]{:S(2)}, u32[]{:S(2)}) %collective-permute-start.15) | collective-permute-done | bytes 57376 | tf_op jit(solution)/shard_map/ppermute | solution.py:184
  51.0 0.6 %collective-permute-done.16.refs_3_ = f32[112,128]{1,0:T(8,128)S(1)} collective-permute-done((f32[112,128]{1,0:T(8,128)S(1)}, f32[112,128]{1,0:T(8,128)S(1)}, u32[]{:S(2)}, u32[]{:S(2)}) %collective-permute-start.16) | collective-permute-done | bytes 57376 | tf_op jit(solution)/shard_map/ppermute | solution.py:184
  51.6 0.2 tm_sums.5
  51.8 1.5 %collective-permute-start.17 = (f32[96,128]{1,0:T(8,128)S(1)}, f32[96,128]{1,0:T(8,128)S(1)}, u32[]{:S(2)}, u32[]{:S(2)}) collective-permute-start(f32[96,128]{1,0:T(8,128)S(1)} %get-tuple-element.23), channel_id=1, source_target_pairs={{0,4},{1,5},{2,6},{3,7},{4,0},{5,1},{6,2},{7,3},{8,12},{9,13},{10,... | collective-permute-start | bytes 147464 | tf_op jit(solution)/shard_map/ppermute | solution.py:184
  53.3 1.5 %collective-permute-start.19 = (f32[64,128]{1,0:T(8,128)S(1)}, f32[64,128]{1,0:T(8,128)S(1)}, u32[]{:S(2)}, u32[]{:S(2)}) collective-permute-start(f32[64,128]{1,0:T(8,128)S(1)} %time_part.5.refs_4_), channel_id=1, source_target_pairs={{0,20},{1,21},{2,22},{3,23},{4,16},{5,17},{6,18},{7,19},{8,28},{9,... | collective-permute-start | bytes 98312 | tf_op jit(solution)/shard_map/ppermute | solution.py:184
  54.8 0.6 collective-permute-start.18
  55.4 0.6 collective-permute-done.17
  56.0 0.1 fusion.14
  56.1 2.1 %collective-permute-done.19 = f32[64,128]{1,0:T(8,128)S(1)} collective-permute-done((f32[64,128]{1,0:T(8,128)S(1)}, f32[64,128]{1,0:T(8,128)S(1)}, u32[]{:S(2)}, u32[]{:S(2)}) %collective-permute-start.19) | collective-permute-done | bytes 32800 | tf_op jit(solution)/shard_map/ppermute | solution.py:184
  58.1 0.9 %collective-permute-done.18 = f32[128,128]{1,0:T(8,128)S(1)} collective-permute-done((f32[128,128]{1,0:T(8,128)S(1)}, f32[128,128]{1,0:T(8,128)S(1)}, u32[]{:S(2)}, u32[]{:S(2)}) %collective-permute-start.18) | collective-permute-done | bytes 65568 | tf_op jit(solution)/shard_map/ppermute | solution.py:184
  59.1 0.1 collective-permute-start.20
  59.1 0.6 %maximum_multiply_fusion.2 = f32[64,64]{1,0:T(8,128)} fusion(f32[32,64]{1,0:T(8,128)S(1)} %get-tuple-element.38, f32[32,64]{1,0:T(8,128)S(1)} %get-tuple-element.37), kind=kLoop, calls=%fused_computation.31 | loop fusion | flops 8192 | bytes 32768 | tf_op jit(solution)/shard_map/div | solution.py:264
  59.8 0.6 %collective-permute-done.20 = f32[128,128]{1,0:T(8,128)S(1)} collective-permute-done((f32[128,128]{1,0:T(8,128)S(1)}, f32[128,128]{1,0:T(8,128)S(1)}, u32[]{:S(2)}, u32[]{:S(2)}) %collective-permute-start.20) | collective-permute-done | bytes 65568 | tf_op jit(solution)/shard_map/ppermute | solution.py:184
  60.4 0.6 %fusion = (f32[128,64]{0,1:T(8,128)}, f32[128,64]{0,1:T(8,128)}) fusion(f32[128,128]{1,0:T(8,128)S(1)} %fusion.11), kind=kLoop, calls=%fused_computation.4 | loop fusion | flops 16384 | bytes 131072 | tf_op jit(solution)/shard_map/transpose | solution.py:271
  (24 shorter events, 0.3 us)
Async XLA Ops:
  3.4 6.8 %collective-permute-start = (f32[112,128]{1,0:T(8,128)S(1)}, f32[112,128]{1,0:T(8,128)S(1)}, u32[]{:S(2)}, u32[]{:S(2)}) collective-permute-start(f32[112,128]{1,0:T(8,128)S(1)} %get-tuple-element.16.refs_0_), channel_id=1, source_target_pairs={{0,1},{1,0},{2,3},{3,2},{4,5},{5,4},{6,7},{7,6},{8,9},{9,8},{10,11... | collective-permute-start | bytes 172040 | tf_op jit(solution)/shard_map/ppermute | solution.py:184
  6.6 6.2 %collective-permute-start.1 = (f32[112,128]{1,0:T(8,128)S(1)}, f32[112,128]{1,0:T(8,128)S(1)}, u32[]{:S(2)}, u32[]{:S(2)}) collective-permute-start(f32[112,128]{1,0:T(8,128)S(1)} %get-tuple-element.16.refs_0_), channel_id=1, source_target_pairs={{0,2},{1,3},{2,0},{3,1},{4,6},{5,7},{6,4},{7,5},{8,10},{9,11},{10,... | collective-permute-start | bytes 172040 | tf_op jit(solution)/shard_map/ppermute | solution.py:184
  9.2 6.0 %collective-permute-start.2 = (f32[112,128]{1,0:T(8,128)S(1)}, f32[112,128]{1,0:T(8,128)S(1)}, u32[]{:S(2)}, u32[]{:S(2)}) collective-permute-start(f32[112,128]{1,0:T(8,128)S(1)} %get-tuple-element.16.refs_0_), channel_id=1, source_target_pairs={{0,3},{1,2},{2,1},{3,0},{4,7},{5,6},{6,5},{7,4},{8,11},{9,10},{10,... | collective-permute-start | bytes 172040 | tf_op jit(solution)/shard_map/ppermute | solution.py:184
  15.3 4.2 %collective-permute-start.3 = (f32[96,128]{1,0:T(8,128)S(1)}, f32[96,128]{1,0:T(8,128)S(1)}, u32[]{:S(2)}, u32[]{:S(2)}) collective-permute-start(f32[96,128]{1,0:T(8,128)S(1)} %get-tuple-element.19), channel_id=1, source_target_pairs={{0,4},{1,5},{2,6},{3,7},{4,0},{5,1},{6,2},{7,3},{8,12},{9,13},{10,... | collective-permute-start | bytes 147464 | tf_op jit(solution)/shard_map/ppermute | solution.py:184
  16.9 4.8 %collective-permute-start.5 = (f32[64,128]{1,0:T(8,128)S(1)}, f32[64,128]{1,0:T(8,128)S(1)}, u32[]{:S(2)}, u32[]{:S(2)}) collective-permute-start(f32[64,128]{1,0:T(8,128)S(1)} %time_part.3.refs_4_), channel_id=1, source_target_pairs={{0,20},{1,21},{2,22},{3,23},{4,16},{5,17},{6,18},{7,19},{8,28},{9,... | collective-permute-start | bytes 98312 | tf_op jit(solution)/shard_map/ppermute | solution.py:184
  18.4 4.3 %collective-permute-start.4 = (f32[128,128]{1,0:T(8,128)S(1)}, f32[128,128]{1,0:T(8,128)S(1)}, u32[]{:S(2)}, u32[]{:S(2)}) collective-permute-start(f32[128,128]{1,0:T(8,128)S(1)} %get-tuple-element.20), channel_id=1, source_target_pairs={{0,16},{1,17},{2,18},{3,19},{4,20},{5,21},{6,22},{7,23},{8,24},{9,... | collective-permute-start | bytes 196616 | tf_op jit(solution)/shard_map/ppermute | solution.py:184
  22.6 1.3 %collective-permute-start.6 = (f32[128,128]{1,0:T(8,128)S(1)}, f32[128,128]{1,0:T(8,128)S(1)}, u32[]{:S(2)}, u32[]{:S(2)}) collective-permute-start(f32[128,128]{1,0:T(8,128)S(1)} %pad_maximum_fusion), channel_id=1, source_target_pairs={{0,8},{1,9},{2,10},{3,11},{4,12},{5,13},{6,14},{7,15},{8,0},{9,1},... | collective-permute-start | bytes 196616 | tf_op jit(solution)/shard_map/ppermute | solution.py:184
  25.2 5.5 %collective-permute-start.7 = (f32[112,128]{1,0:T(8,128)S(1)}, f32[112,128]{1,0:T(8,128)S(1)}, u32[]{:S(2)}, u32[]{:S(2)}) collective-permute-start(f32[112,128]{1,0:T(8,128)S(1)} %src_dst_part.2.refs_0_), channel_id=1, source_target_pairs={{0,1},{1,0},{2,3},{3,2},{4,5},{5,4},{6,7},{7,6},{8,9},{9,8},{10,11... | collective-permute-start | bytes 172040 | tf_op jit(solution)/shard_map/ppermute | solution.py:184
  25.3 8.1 %collective-permute-start.8 = (f32[112,128]{1,0:T(8,128)S(1)}, f32[112,128]{1,0:T(8,128)S(1)}, u32[]{:S(2)}, u32[]{:S(2)}) collective-permute-start(f32[112,128]{1,0:T(8,128)S(1)} %src_dst_part.2.refs_0_), channel_id=1, source_target_pairs={{0,2},{1,3},{2,0},{3,1},{4,6},{5,7},{6,4},{7,5},{8,10},{9,11},{10,... | collective-permute-start | bytes 172040 | tf_op jit(solution)/shard_map/ppermute | solution.py:184
  27.1 6.4 %collective-permute-start.9 = (f32[112,128]{1,0:T(8,128)S(1)}, f32[112,128]{1,0:T(8,128)S(1)}, u32[]{:S(2)}, u32[]{:S(2)}) collective-permute-start(f32[112,128]{1,0:T(8,128)S(1)} %src_dst_part.2.refs_0_), channel_id=1, source_target_pairs={{0,3},{1,2},{2,1},{3,0},{4,7},{5,6},{6,5},{7,4},{8,11},{9,10},{10,... | collective-permute-start | bytes 172040 | tf_op jit(solution)/shard_map/ppermute | solution.py:184
  33.6 4.3 %collective-permute-start.10 = (f32[96,128]{1,0:T(8,128)S(1)}, f32[96,128]{1,0:T(8,128)S(1)}, u32[]{:S(2)}, u32[]{:S(2)}) collective-permute-start(f32[96,128]{1,0:T(8,128)S(1)} %get-tuple-element.21), channel_id=1, source_target_pairs={{0,4},{1,5},{2,6},{3,7},{4,0},{5,1},{6,2},{7,3},{8,12},{9,13},{10,... | collective-permute-start | bytes 147464 | tf_op jit(solution)/shard_map/ppermute | solution.py:184
  35.2 4.8 %collective-permute-start.12 = (f32[64,128]{1,0:T(8,128)S(1)}, f32[64,128]{1,0:T(8,128)S(1)}, u32[]{:S(2)}, u32[]{:S(2)}) collective-permute-start(f32[64,128]{1,0:T(8,128)S(1)} %time_part.4.refs_4_), channel_id=1, source_target_pairs={{0,20},{1,21},{2,22},{3,23},{4,16},{5,17},{6,18},{7,19},{8,28},{9,... | collective-permute-start | bytes 98312 | tf_op jit(solution)/shard_map/ppermute | solution.py:184
  35.7 4.3 %collective-permute-start.11 = (f32[128,128]{1,0:T(8,128)S(1)}, f32[128,128]{1,0:T(8,128)S(1)}, u32[]{:S(2)}, u32[]{:S(2)}) collective-permute-start(f32[128,128]{1,0:T(8,128)S(1)} %get-tuple-element.22), channel_id=1, source_target_pairs={{0,16},{1,17},{2,18},{3,19},{4,20},{5,21},{6,22},{7,23},{8,24},{9,... | collective-permute-start | bytes 196616 | tf_op jit(solution)/shard_map/ppermute | solution.py:184
  40.0 1.3 %collective-permute-start.13 = (f32[128,128]{1,0:T(8,128)S(1)}, f32[128,128]{1,0:T(8,128)S(1)}, u32[]{:S(2)}, u32[]{:S(2)}) collective-permute-start(f32[128,128]{1,0:T(8,128)S(1)} %pad_maximum_fusion.1), channel_id=1, source_target_pairs={{0,8},{1,9},{2,10},{3,11},{4,12},{5,13},{6,14},{7,15},{8,0},{9,1},... | collective-permute-start | bytes 196616 | tf_op jit(solution)/shard_map/ppermute | solution.py:184
  42.6 5.5 %collective-permute-start.14 = (f32[112,128]{1,0:T(8,128)S(1)}, f32[112,128]{1,0:T(8,128)S(1)}, u32[]{:S(2)}, u32[]{:S(2)}) collective-permute-start(f32[112,128]{1,0:T(8,128)S(1)} %src_dst_part.3.refs_0_), channel_id=1, source_target_pairs={{0,1},{1,0},{2,3},{3,2},{4,5},{5,4},{6,7},{7,6},{8,9},{9,8},{10,11... | collective-permute-start | bytes 172040 | tf_op jit(solution)/shard_map/ppermute | solution.py:184
  43.9 7.1 %collective-permute-start.15 = (f32[112,128]{1,0:T(8,128)S(1)}, f32[112,128]{1,0:T(8,128)S(1)}, u32[]{:S(2)}, u32[]{:S(2)}) collective-permute-start(f32[112,128]{1,0:T(8,128)S(1)} %src_dst_part.3.refs_0_), channel_id=1, source_target_pairs={{0,2},{1,3},{2,0},{3,1},{4,6},{5,7},{6,4},{7,5},{8,10},{9,11},{10,... | collective-permute-start | bytes 172040 | tf_op jit(solution)/shard_map/ppermute | solution.py:184
  45.6 6.1 %collective-permute-start.16 = (f32[112,128]{1,0:T(8,128)S(1)}, f32[112,128]{1,0:T(8,128)S(1)}, u32[]{:S(2)}, u32[]{:S(2)}) collective-permute-start(f32[112,128]{1,0:T(8,128)S(1)} %src_dst_part.3.refs_0_), channel_id=1, source_target_pairs={{0,3},{1,2},{2,1},{3,0},{4,7},{5,6},{6,5},{7,4},{8,11},{9,10},{10,... | collective-permute-start | bytes 172040 | tf_op jit(solution)/shard_map/ppermute | solution.py:184
  51.8 4.2 %collective-permute-start.17 = (f32[96,128]{1,0:T(8,128)S(1)}, f32[96,128]{1,0:T(8,128)S(1)}, u32[]{:S(2)}, u32[]{:S(2)}) collective-permute-start(f32[96,128]{1,0:T(8,128)S(1)} %get-tuple-element.23), channel_id=1, source_target_pairs={{0,4},{1,5},{2,6},{3,7},{4,0},{5,1},{6,2},{7,3},{8,12},{9,13},{10,... | collective-permute-start | bytes 147464 | tf_op jit(solution)/shard_map/ppermute | solution.py:184
  53.3 4.8 %collective-permute-start.19 = (f32[64,128]{1,0:T(8,128)S(1)}, f32[64,128]{1,0:T(8,128)S(1)}, u32[]{:S(2)}, u32[]{:S(2)}) collective-permute-start(f32[64,128]{1,0:T(8,128)S(1)} %time_part.5.refs_4_), channel_id=1, source_target_pairs={{0,20},{1,21},{2,22},{3,23},{4,16},{5,17},{6,18},{7,19},{8,28},{9,... | collective-permute-start | bytes 98312 | tf_op jit(solution)/shard_map/ppermute | solution.py:184
  54.8 4.3 %collective-permute-start.18 = (f32[128,128]{1,0:T(8,128)S(1)}, f32[128,128]{1,0:T(8,128)S(1)}, u32[]{:S(2)}, u32[]{:S(2)}) collective-permute-start(f32[128,128]{1,0:T(8,128)S(1)} %get-tuple-element.24), channel_id=1, source_target_pairs={{0,16},{1,17},{2,18},{3,19},{4,20},{5,21},{6,22},{7,23},{8,24},{9,... | collective-permute-start | bytes 196616 | tf_op jit(solution)/shard_map/ppermute | solution.py:184
  59.1 1.3 %collective-permute-start.20 = (f32[128,128]{1,0:T(8,128)S(1)}, f32[128,128]{1,0:T(8,128)S(1)}, u32[]{:S(2)}, u32[]{:S(2)}) collective-permute-start(f32[128,128]{1,0:T(8,128)S(1)} %pad_maximum_fusion.2), channel_id=1, source_target_pairs={{0,8},{1,9},{2,10},{3,11},{4,12},{5,13},{6,14},{7,15},{8,0},{9,1},... | collective-permute-start | bytes 196616 | tf_op jit(solution)/shard_map/ppermute | solution.py:184
where the time goes:
time: 61.2 us; the launch traced here: 61 us
  starting transfers between devices  25.5 us (42%)
  waiting for transfers between devices  24.2 us (40%)
  Pallas kernels  8.88 us (15%)
  other arithmetic  1.4 us (2%)
  between operations  0.83 us (1%)
    ppermute x21, starting transfers between devices, exchanged(): return lax.ppermute(x, AXES, route)  25.5 us
    ppermute x21, waiting for transfers between devices, exchanged(): return lax.ppermute(x, AXES, route)  24.2 us
    pallas_call x3, Pallas kernels, on_device(): time_part = second_kernel(traffic, src_now, dst_now, time_now)  3.12 us
    pallas_call x1, Pallas kernels, on_device(): mixed, traffic, src_now, dst_now, time_now = zero_kernel(*given)  2.81 us
    pallas_call x2, Pallas kernels, on_device(): mixed = first_kernel(traffic, src_now, dst_now, time_now)  2.44 us
  transfers between devices with their start and end apart: 21, of which 16 were waited for; matrix products, arithmetic and copies ran while one was open for 1% of the time, Pallas kernels for 5%

commit v1 on v0

--- a/solution.py
+++ b/solution.py
@@ -49,14 +49,17 @@
     return x if fold == 1 else jnp.concatenate([x[:, i * columns : (i + 1) * columns] for i in range(fold)], 0)
 
 
-def place_of(count):
-    place = lax.axis_index("src") * (lax.axis_size("dst") // 2) + lax.axis_index("dst") // 2
+def place_of(count, core=0):
+    place = (lax.axis_index("src") ^ core) * (lax.axis_size("dst") // 2) + lax.axis_index("dst") // 2
     return jnp.minimum(place, count - 1), place < count
 
 
 def src_dst_part(slice_rows, traffic, src_now, dst_now, time_now, time, out, ready=None):
     rank = src_now.shape[1]
     src_rows, dst_rows, time_rows = traffic.shape
+    time_gram = gram(time_now)
+    src_model = times(src_now, gram(dst_now) * time_gram)
+    dst_model = times(gram(src_now.T) * time_gram, dst_now)
     time_halves = halves(time_now)
     dst_wide = jnp.concatenate([dst_now, dst_now], 0).T
     src_wide = jnp.concatenate([src_now, src_now], 1)
@@ -74,9 +77,8 @@
             rows.append(jnp.sum(part * dst_wide, axis=0, keepdims=True))
     src_sum = jnp.concatenate(rows, 0)
     dst_seen = (dst_sum[:, :rank] + dst_sum[:, rank:]).T
-    time_gram = gram(time_now)
-    src_part = times(src_now, gram(dst_now) * time_gram) - (src_sum[:, :rank] + src_sum[:, rank:])
-    dst_part = times(gram(src_now.T) * time_gram, dst_now) - dst_seen
+    src_part = src_model - (src_sum[:, :rank] + src_sum[:, rank:])
+    dst_part = dst_model - dst_seen
     src_packed = packed(src_part)
     top = src_packed.shape[0]
     out[:top] = src_packed
@@ -140,7 +142,7 @@
 
 
 def smooth_kernel(slice_rows, src_top, blocks, *refs):
-    held, time_part, src_time_out, dst_time_out = refs[:blocks], refs[blocks], refs[-2], refs[-1]
+    held, time_part, src_time_out, dst_out = refs[:blocks], refs[blocks], *refs[-2:]
     rank, time_rows = time_part.shape
     here = lax.axis_index("tm")
     total = held[0][: src_top + rank]
@@ -148,7 +150,7 @@
         total = total + other[: src_top + rank]
     src_time_out[:src_top] = total[:src_top]
     src_time_out[src_top:] = time_part[...]
-    dst_time_out[:rank] = total[src_top:]
+    dst_out[:rank] = total[src_top:]
     slices = [h[src_top + rank :] for h in held]
     ordered = []
     for block in range(blocks):
@@ -165,11 +167,17 @@
     mine = smooth[:, :time_rows]
     for block in range(1, blocks):
         mine = jnp.where(here == block, smooth[:, block * time_rows : (block + 1) * time_rows], mine)
-    dst_time_out[rank:] = time_part[...]
-    place, smooths = place_of(rank // slice_rows)
-    mine = jnp.where(smooths, mine, 0.0)
-    start = pl.multiple_of(rank + place * slice_rows, slice_rows)
-    dst_time_out[pl.ds(start, slice_rows)] = dst_time_out[pl.ds(start, slice_rows)] + mine
+    dst_out[rank:] = jnp.where(place_of(rank // slice_rows)[1], mine, 0.0)
+
+
+def join_kernel(slice_rows, own, other, time_part, out):
+    rank = time_part.shape[0]
+    out[:rank] = own[:rank] + other[:rank]
+    out[rank:] = time_part[...]
+    for core, given in enumerate((own, other)):
+        place = place_of(rank // slice_rows, core)[0]
+        rows = pl.ds(pl.multiple_of(rank + place * slice_rows, slice_rows), slice_rows)
+        out[rows] = out[rows] + given[rank:]
 
 
 def exchanged(x, src_mask, dst_mask, tm_mask):
@@ -226,12 +234,20 @@
         functools.partial(smooth_kernel, slice_rows, src_top, tm_size),
         out_shape=(
             jax.ShapeDtypeStruct((src_top + rank, LANES), f32),
-            jax.ShapeDtypeStruct((2 * rank, LANES), f32),
+            jax.ShapeDtypeStruct((rank + slice_rows, dst_rows), f32),
         ),
         in_specs=[VMEM] * (tm_size + 1),
-        out_specs=(VMEM, VMEM),
+        out_specs=(VMEM,) * 2,
         compiler_params=PARAMS,
         name="tm_sums",
+    )
+    join = pl.pallas_call(
+        functools.partial(join_kernel, slice_rows),
+        out_shape=jax.ShapeDtypeStruct((2 * rank, LANES), f32),
+        in_specs=[VMEM] * 3,
+        out_specs=VMEM,
+        compiler_params=PARAMS,
+        name="join",
     )
     for iteration in range(STEPS):
         if iteration == 0:
@@ -240,10 +256,15 @@
             mixed, traffic, src_now, dst_now, time_now = zero_kernel(*given)
         else:
             mixed = first_kernel(traffic, src_now, dst_now, time_now)
-        others = [exchanged(mixed, 0, 0, mask) for mask in range(1, tm_size)]
+        others = []
+        for mask in range(1, tm_size):
+            others.append(exchanged(mixed, 0, 0, mask))
         time_part = second_kernel(traffic, src_now, dst_now, time_now)
+        time_part = time_part + exchanged(time_part, 1, 0, 0)
         add_time = exchanged(time_part, 2, 1, 0)
-        src_time, dst_time = third_kernel(mixed, *others, time_part)
+        src_time, dst_smooth = third_kernel(mixed, *others, time_part)
+        other_smooth = exchanged(dst_smooth, 1, 0, 0)
+        dst_time = join(dst_smooth, other_smooth, time_part)
         src_mask, dst_mask = 2, 1
         while src_mask < src_size or dst_mask < dst_size:
             if src_mask > 2:
@@ -252,15 +273,14 @@
                 add_time = exchanged(dst_time[rank:], src_mask, dst_mask, 0) if both else 0.0
             src_sum = src_time[:src_top]
             add_dst = 0.0
+            if dst_mask < dst_size:
+                other = exchanged(src_time, 0, dst_mask, 0)
+                src_sum, add_time = src_sum + other[:src_top], add_time + other[src_top:]
             if src_mask < src_size:
                 other = exchanged(dst_time, src_mask, 0, 0)
                 add_dst, add_time = other[:rank], add_time + other[rank:]
-            if dst_mask < dst_size:
-                other = exchanged(src_time, 0, dst_mask, 0)
-                src_sum, add_time = src_sum + other[:src_top], add_time + other[src_top:]
             dst_time = jnp.concatenate([dst_time[:rank] + add_dst, dst_time[rank:] + add_time], 0)
             src_mask, dst_mask = src_mask * 2, dst_mask * 2
-        dst_time = dst_time + exchanged(dst_time, 1, 0, 0)
         grad_src = unpacked(src_sum, rank) / rank
         grad_dst = dst_time[:rank] / rank
         grad_time = dst_time[rank:] / rank

time: 61.2 us -> 56.4 us (0.922)
  waiting for transfers between devices: 24.2 us -> 17.8 us
  starting transfers between devices: 25.5 us -> 26.9 us
    ppermute x21 -> x24, waiting for transfers between devices: 24.2 us -> 17.8 us  [exchanged(): return lax.ppermute(x, AXES, route)]
    ppermute x21 -> x24, starting transfers between devices: 25.5 us -> 26.9 us  [exchanged(): return lax.ppermute(x, AXES, route)]
  transfers between devices with their start and end apart: 21 -> 24, of which waited for: 16 -> 14; matrix products, arithmetic and copies ran while one was open for 1% -> 2% of each run, Pallas kernels for 5% -> 6%
where the time goes in v1:
time: 56.4 us; the launch traced here: 56.3 us
  starting transfers between devices  26.9 us (48%)
  waiting for transfers between devices  17.8 us (32%)
  Pallas kernels  9.18 us (16%)
  other arithmetic  1.36 us (2%)
  between operations  0.8 us (1%)
    ppermute x24, starting transfers between devices, exchanged(): return lax.ppermute(x, AXES, route)  26.9 us
    ppermute x24, waiting for transfers between devices, exchanged(): return lax.ppermute(x, AXES, route)  17.8 us
    pallas_call x3, Pallas kernels, on_device(): time_part = second_kernel(traffic, src_now, dst_now, time_now)  3.12 us
    pallas_call x1, Pallas kernels, on_device(): mixed, traffic, src_now, dst_now, time_now = zero_kernel(*given)  2.8 us
    pallas_call x2, Pallas kernels, on_device(): mixed = first_kernel(traffic, src_now, dst_now, time_now)  2.67 us
  transfers between devices with their start and end apart: 24, of which 14 were waited for; matrix products, arithmetic and copies ran while one was open for 2% of the time, Pallas kernels for 6%

profile of v1, /device:TPU:0, one launch (start us, length us, event | category | flops | bytes accessed | tf_op | source)
XLA Modules:
  0.0 56.3 jit_solution(15596254768331857902)
XLA Ops:
  0.6 2.8 %entry.1 = (f32[112,128]{1,0:T(8,128)S(1)}, bf16[64,128,128]{2,1,0:T(8,128)(2,1)S(1)}, f32[64,64]{1,0:T(8,128)S(1)}, f32[64,128]{1,0:T(8,128)S(1)}, f32[64,128]{1,0:T(8,128)S(1)}) custom-call(bf16[64,128,128]{2,1,0:T(8,128)(2,1)} %traffic_in.1, f32[64,64]{1,0:T(8,128)} %src_in.1, f32[64,128]{1,0:T(8,128)} %bitcast.6, f32[64,128]{1,0:T(8,128)} %bitcast.7), custom_call_target="tpu_custom_call" | custom-call | tf_op jit(solution)/shard_map/entry/pallas_call | solution.py:256
  3.4 3.1 %collective-permute-start = (f32[112,128]{1,0:T(8,128)S(1)}, f32[112,128]{1,0:T(8,128)S(1)}, u32[]{:S(2)}, u32[]{:S(2)}) collective-permute-start(f32[112,128]{1,0:T(8,128)S(1)} %get-tuple-element.16.refs_0_), channel_id=1, source_target_pairs={{0,1},{1,0},{2,3},{3,2},{4,5},{5,4},{6,7},{7,6},{8,9},{9,8},{10,11... | collective-permute-start | bytes 172040 | tf_op jit(solution)/shard_map/ppermute | solution.py:192
  6.5 2.6 %collective-permute-start.1 = (f32[112,128]{1,0:T(8,128)S(1)}, f32[112,128]{1,0:T(8,128)S(1)}, u32[]{:S(2)}, u32[]{:S(2)}) collective-permute-start(f32[112,128]{1,0:T(8,128)S(1)} %get-tuple-element.16.refs_0_), channel_id=1, source_target_pairs={{0,2},{1,3},{2,0},{3,1},{4,6},{5,7},{6,4},{7,5},{8,10},{9,11},{10,... | collective-permute-start | bytes 172040 | tf_op jit(solution)/shard_map/ppermute | solution.py:192
  9.2 1.0 %time_part.3 = f32[64,128]{1,0:T(8,128)S(1)} custom-call(bf16[64,128,128]{2,1,0:T(8,128)(2,1)S(1)} %get-tuple-element.14.traffic, f32[64,64]{1,0:T(8,128)S(1)} %get-tuple-element.15.src, f32[64,128]{1,0:T(8,128)S(1)} %get-tuple-element.17.dst, f32[64,128]{1,0:T(8,128)S(1)} %get-tuple-element.18.time), custom_call_target="tpu_custom_call" | custom-call | tf_op jit(solution)/shard_map/time_part/pallas_call | solution.py:262
  10.2 0.1 collective-permute-start.3
  10.3 1.2 %collective-permute-done.3 = f32[64,128]{1,0:T(8,128)S(1)} collective-permute-done((f32[64,128]{1,0:T(8,128)S(1)}, f32[64,128]{1,0:T(8,128)S(1)}, u32[]{:S(2)}, u32[]{:S(2)}) %collective-permute-start.3) | collective-permute-done | bytes 32800 | tf_op jit(solution)/shard_map/ppermute | solution.py:192
  11.5 1.3 %collective-permute-done.1.refs_2_ = f32[112,128]{1,0:T(8,128)S(1)} collective-permute-done((f32[112,128]{1,0:T(8,128)S(1)}, f32[112,128]{1,0:T(8,128)S(1)}, u32[]{:S(2)}, u32[]{:S(2)}) %collective-permute-start.1) | collective-permute-done | bytes 57376 | tf_op jit(solution)/shard_map/ppermute | solution.py:192
  12.7 2.4 %collective-permute-done.2.refs_3_ = f32[112,128]{1,0:T(8,128)S(1)} collective-permute-done((f32[112,128]{1,0:T(8,128)S(1)}, f32[112,128]{1,0:T(8,128)S(1)}, u32[]{:S(2)}, u32[]{:S(2)}) %collective-permute-start.2) | collective-permute-done | bytes 57376 | tf_op jit(solution)/shard_map/ppermute | solution.py:192
  15.1 0.2 tm_sums.3
  15.3 1.6 %collective-permute-start.4 = (f32[96,128]{1,0:T(8,128)S(1)}, f32[96,128]{1,0:T(8,128)S(1)}, u32[]{:S(2)}, u32[]{:S(2)}) collective-permute-start(f32[96,128]{1,0:T(8,128)S(1)} %get-tuple-element.19), channel_id=1, source_target_pairs={{0,4},{1,5},{2,6},{3,7},{4,0},{5,1},{6,2},{7,3},{8,12},{9,13},{10,... | collective-permute-start | bytes 147464 | tf_op jit(solution)/shard_map/ppermute | solution.py:192
  16.9 1.4 %collective-permute-start.7 = (f32[64,128]{1,0:T(8,128)S(1)}, f32[64,128]{1,0:T(8,128)S(1)}, u32[]{:S(2)}, u32[]{:S(2)}) collective-permute-start(f32[64,128]{1,0:T(8,128)S(1)} %add.54.refs_4_.time_part), channel_id=1, source_target_pairs={{0,20},{1,21},{2,22},{3,23},{4,16},{5,17},{6,18},{7,19},{8,28},{9,... | collective-permute-start | bytes 98312 | tf_op jit(solution)/shard_map/ppermute | solution.py:192
  18.3 1.4 %collective-permute-start.6 = (f32[128,128]{1,0:T(8,128)S(1)}, f32[128,128]{1,0:T(8,128)S(1)}, u32[]{:S(2)}, u32[]{:S(2)}) collective-permute-start(f32[128,128]{1,0:T(8,128)S(1)} %join.3), channel_id=1, source_target_pairs={{0,16},{1,17},{2,18},{3,19},{4,20},{5,21},{6,22},{7,23},{8,24},{9,... | collective-permute-start | bytes 196616 | tf_op jit(solution)/shard_map/ppermute | solution.py:192
  19.7 0.1 fusion.19
  19.8 1.9 %collective-permute-done.7 = f32[64,128]{1,0:T(8,128)S(1)} collective-permute-done((f32[64,128]{1,0:T(8,128)S(1)}, f32[64,128]{1,0:T(8,128)S(1)}, u32[]{:S(2)}, u32[]{:S(2)}) %collective-permute-start.7) | collective-permute-done | bytes 32800 | tf_op jit(solution)/shard_map/ppermute | solution.py:192
  21.7 0.9 %collective-permute-done.6 = f32[128,128]{1,0:T(8,128)S(1)} collective-permute-done((f32[128,128]{1,0:T(8,128)S(1)}, f32[128,128]{1,0:T(8,128)S(1)}, u32[]{:S(2)}, u32[]{:S(2)}) %collective-permute-start.6) | collective-permute-done | bytes 65568 | tf_op jit(solution)/shard_map/ppermute | solution.py:192
  22.7 1.3 %src_dst_part.2.refs_0_ = f32[112,128]{1,0:T(8,128)S(1)} custom-call(bf16[64,128,128]{2,1,0:T(8,128)(2,1)S(1)} %get-tuple-element.14.traffic, f32[64,64]{1,0:T(8,128)S(1)} %fusion.15.src, f32[64,128]{1,0:T(8,128)S(1)} %get-tuple-element.30.dst, f32[64,128]{1,0:T(8,128)S(1)} %get-tuple-element.29.time), custom_call_target="tpu_custom_call" | custom-call | tf_op jit(solution)/shard_map/src_dst_part/pallas_call | solution.py:258
  24.0 1.3 %collective-permute-start.10 = (f32[112,128]{1,0:T(8,128)S(1)}, f32[112,128]{1,0:T(8,128)S(1)}, u32[]{:S(2)}, u32[]{:S(2)}) collective-permute-start(f32[112,128]{1,0:T(8,128)S(1)} %src_dst_part.2.refs_0_), channel_id=1, source_target_pairs={{0,3},{1,2},{2,1},{3,0},{4,7},{5,6},{6,5},{7,4},{8,11},{9,10},{10,... | collective-permute-start | bytes 172040 | tf_op jit(solution)/shard_map/ppermute | solution.py:192
  25.3 0.3 collective-permute-start.8
  25.6 2.9 %collective-permute-start.9 = (f32[112,128]{1,0:T(8,128)S(1)}, f32[112,128]{1,0:T(8,128)S(1)}, u32[]{:S(2)}, u32[]{:S(2)}) collective-permute-start(f32[112,128]{1,0:T(8,128)S(1)} %src_dst_part.2.refs_0_), channel_id=1, source_target_pairs={{0,2},{1,3},{2,0},{3,1},{4,6},{5,7},{6,4},{7,5},{8,10},{9,11},{10,... | collective-permute-start | bytes 172040 | tf_op jit(solution)/shard_map/ppermute | solution.py:192
  28.5 1.0 %time_part.4 = f32[64,128]{1,0:T(8,128)S(1)} custom-call(bf16[64,128,128]{2,1,0:T(8,128)(2,1)S(1)} %get-tuple-element.14.traffic, f32[64,64]{1,0:T(8,128)S(1)} %fusion.15.src, f32[64,128]{1,0:T(8,128)S(1)} %get-tuple-element.30.dst, f32[64,128]{1,0:T(8,128)S(1)} %get-tuple-element.29.time), custom_call_target="tpu_custom_call" | custom-call | tf_op jit(solution)/shard_map/time_part/pallas_call | solution.py:262
  29.5 0.1 collective-permute-start.11
  29.6 1.2 %collective-permute-done.11 = f32[64,128]{1,0:T(8,128)S(1)} collective-permute-done((f32[64,128]{1,0:T(8,128)S(1)}, f32[64,128]{1,0:T(8,128)S(1)}, u32[]{:S(2)}, u32[]{:S(2)}) %collective-permute-start.11) | collective-permute-done | bytes 32800 | tf_op jit(solution)/shard_map/ppermute | solution.py:192
  30.8 0.2 tm_sums.4
  31.0 1.6 %collective-permute-start.12 = (f32[96,128]{1,0:T(8,128)S(1)}, f32[96,128]{1,0:T(8,128)S(1)}, u32[]{:S(2)}, u32[]{:S(2)}) collective-permute-start(f32[96,128]{1,0:T(8,128)S(1)} %get-tuple-element.21), channel_id=1, source_target_pairs={{0,4},{1,5},{2,6},{3,7},{4,0},{5,1},{6,2},{7,3},{8,12},{9,13},{10,... | collective-permute-start | bytes 147464 | tf_op jit(solution)/shard_map/ppermute | solution.py:192
  32.6 1.3 %collective-permute-start.15 = (f32[64,128]{1,0:T(8,128)S(1)}, f32[64,128]{1,0:T(8,128)S(1)}, u32[]{:S(2)}, u32[]{:S(2)}) collective-permute-start(f32[64,128]{1,0:T(8,128)S(1)} %add.60.refs_4_.time_part), channel_id=1, source_target_pairs={{0,20},{1,21},{2,22},{3,23},{4,16},{5,17},{6,18},{7,19},{8,28},{9,... | collective-permute-start | bytes 98312 | tf_op jit(solution)/shard_map/ppermute | solution.py:192
  33.9 1.3 %collective-permute-start.14 = (f32[128,128]{1,0:T(8,128)S(1)}, f32[128,128]{1,0:T(8,128)S(1)}, u32[]{:S(2)}, u32[]{:S(2)}) collective-permute-start(f32[128,128]{1,0:T(8,128)S(1)} %join.4), channel_id=1, source_target_pairs={{0,16},{1,17},{2,18},{3,19},{4,20},{5,21},{6,22},{7,23},{8,24},{9,... | collective-permute-start | bytes 196616 | tf_op jit(solution)/shard_map/ppermute | solution.py:192
  35.2 0.1 fusion.18
  35.3 2.1 %collective-permute-done.15 = f32[64,128]{1,0:T(8,128)S(1)} collective-permute-done((f32[64,128]{1,0:T(8,128)S(1)}, f32[64,128]{1,0:T(8,128)S(1)}, u32[]{:S(2)}, u32[]{:S(2)}) %collective-permute-start.15) | collective-permute-done | bytes 32800 | tf_op jit(solution)/shard_map/ppermute | solution.py:192
  37.4 0.8 %collective-permute-done.14 = f32[128,128]{1,0:T(8,128)S(1)} collective-permute-done((f32[128,128]{1,0:T(8,128)S(1)}, f32[128,128]{1,0:T(8,128)S(1)}, u32[]{:S(2)}, u32[]{:S(2)}) %collective-permute-start.14) | collective-permute-done | bytes 65568 | tf_op jit(solution)/shard_map/ppermute | solution.py:192
  38.3 1.3 %src_dst_part.3.refs_0_ = f32[112,128]{1,0:T(8,128)S(1)} custom-call(bf16[64,128,128]{2,1,0:T(8,128)(2,1)S(1)} %get-tuple-element.14.traffic, f32[64,64]{1,0:T(8,128)S(1)} %fusion.16.src, f32[64,128]{1,0:T(8,128)S(1)} %get-tuple-element.28.dst, f32[64,128]{1,0:T(8,128)S(1)} %get-tuple-element.27.time), custom_call_target="tpu_custom_call" | custom-call | tf_op jit(solution)/shard_map/src_dst_part/pallas_call | solution.py:258
  39.6 1.6 %collective-permute-start.16 = (f32[112,128]{1,0:T(8,128)S(1)}, f32[112,128]{1,0:T(8,128)S(1)}, u32[]{:S(2)}, u32[]{:S(2)}) collective-permute-start(f32[112,128]{1,0:T(8,128)S(1)} %src_dst_part.3.refs_0_), channel_id=1, source_target_pairs={{0,1},{1,0},{2,3},{3,2},{4,5},{5,4},{6,7},{7,6},{8,9},{9,8},{10,11... | collective-permute-start | bytes 172040 | tf_op jit(solution)/shard_map/ppermute | solution.py:192
  41.3 1.3 %collective-permute-start.17 = (f32[112,128]{1,0:T(8,128)S(1)}, f32[112,128]{1,0:T(8,128)S(1)}, u32[]{:S(2)}, u32[]{:S(2)}) collective-permute-start(f32[112,128]{1,0:T(8,128)S(1)} %src_dst_part.3.refs_0_), channel_id=1, source_target_pairs={{0,2},{1,3},{2,0},{3,1},{4,6},{5,7},{6,4},{7,5},{8,10},{9,11},{10,... | collective-permute-start | bytes 172040 | tf_op jit(solution)/shard_map/ppermute | solution.py:192
  42.5 1.5 %collective-permute-start.18 = (f32[112,128]{1,0:T(8,128)S(1)}, f32[112,128]{1,0:T(8,128)S(1)}, u32[]{:S(2)}, u32[]{:S(2)}) collective-permute-start(f32[112,128]{1,0:T(8,128)S(1)} %src_dst_part.3.refs_0_), channel_id=1, source_target_pairs={{0,3},{1,2},{2,1},{3,0},{4,7},{5,6},{6,5},{7,4},{8,11},{9,10},{10,... | collective-permute-start | bytes 172040 | tf_op jit(solution)/shard_map/ppermute | solution.py:192
  44.1 1.0 %time_part.5 = f32[64,128]{1,0:T(8,128)S(1)} custom-call(bf16[64,128,128]{2,1,0:T(8,128)(2,1)S(1)} %get-tuple-element.14.traffic, f32[64,64]{1,0:T(8,128)S(1)} %fusion.16.src, f32[64,128]{1,0:T(8,128)S(1)} %get-tuple-element.28.dst, f32[64,128]{1,0:T(8,128)S(1)} %get-tuple-element.27.time), custom_call_target="tpu_custom_call" | custom-call | tf_op jit(solution)/shard_map/time_part/pallas_call | solution.py:262
  45.1 0.1 collective-permute-start.19
  45.2 1.2 %collective-permute-done.19 = f32[64,128]{1,0:T(8,128)S(1)} collective-permute-done((f32[64,128]{1,0:T(8,128)S(1)}, f32[64,128]{1,0:T(8,128)S(1)}, u32[]{:S(2)}, u32[]{:S(2)}) %collective-permute-start.19) | collective-permute-done | bytes 32800 | tf_op jit(solution)/shard_map/ppermute | solution.py:192
  46.4 1.3 %collective-permute-done.17.refs_2_ = f32[112,128]{1,0:T(8,128)S(1)} collective-permute-done((f32[112,128]{1,0:T(8,128)S(1)}, f32[112,128]{1,0:T(8,128)S(1)}, u32[]{:S(2)}, u32[]{:S(2)}) %collective-permute-start.17) | collective-permute-done | bytes 57376 | tf_op jit(solution)/shard_map/ppermute | solution.py:192
  47.7 0.9 %collective-permute-done.18.refs_3_ = f32[112,128]{1,0:T(8,128)S(1)} collective-permute-done((f32[112,128]{1,0:T(8,128)S(1)}, f32[112,128]{1,0:T(8,128)S(1)}, u32[]{:S(2)}, u32[]{:S(2)}) %collective-permute-start.18) | collective-permute-done | bytes 57376 | tf_op jit(solution)/shard_map/ppermute | solution.py:192
  48.6 0.2 tm_sums.5
  48.8 1.2 %collective-permute-start.20 = (f32[96,128]{1,0:T(8,128)S(1)}, f32[96,128]{1,0:T(8,128)S(1)}, u32[]{:S(2)}, u32[]{:S(2)}) collective-permute-start(f32[96,128]{1,0:T(8,128)S(1)} %get-tuple-element.23), channel_id=1, source_target_pairs={{0,4},{1,5},{2,6},{3,7},{4,0},{5,1},{6,2},{7,3},{8,12},{9,13},{10,... | collective-permute-start | bytes 147464 | tf_op jit(solution)/shard_map/ppermute | solution.py:192
  50.0 1.3 %collective-permute-start.23 = (f32[64,128]{1,0:T(8,128)S(1)}, f32[64,128]{1,0:T(8,128)S(1)}, u32[]{:S(2)}, u32[]{:S(2)}) collective-permute-start(f32[64,128]{1,0:T(8,128)S(1)} %add.66.refs_4_.time_part), channel_id=1, source_target_pairs={{0,20},{1,21},{2,22},{3,23},{4,16},{5,17},{6,18},{7,19},{8,28},{9,... | collective-permute-start | bytes 98312 | tf_op jit(solution)/shard_map/ppermute | solution.py:192
  51.3 1.1 %collective-permute-start.22 = (f32[128,128]{1,0:T(8,128)S(1)}, f32[128,128]{1,0:T(8,128)S(1)}, u32[]{:S(2)}, u32[]{:S(2)}) collective-permute-start(f32[128,128]{1,0:T(8,128)S(1)} %join.5), channel_id=1, source_target_pairs={{0,16},{1,17},{2,18},{3,19},{4,20},{5,21},{6,22},{7,23},{8,24},{9,... | collective-permute-start | bytes 196616 | tf_op jit(solution)/shard_map/ppermute | solution.py:192
  52.4 0.5 collective-permute-done.20
  53.0 0.1 fusion.17
  53.0 0.6 %maximum_multiply_fusion.2 = f32[64,64]{1,0:T(8,128)} fusion(f32[32,64]{1,0:T(8,128)S(1)} %get-tuple-element.32, f32[32,64]{1,0:T(8,128)S(1)} %get-tuple-element.31), kind=kLoop, calls=%fused_computation.28 | loop fusion | flops 8192 | bytes 32768 | tf_op jit(solution)/shard_map/div | solution.py:284
  53.7 1.2 %collective-permute-done.23 = f32[64,128]{1,0:T(8,128)S(1)} collective-permute-done((f32[64,128]{1,0:T(8,128)S(1)}, f32[64,128]{1,0:T(8,128)S(1)}, u32[]{:S(2)}, u32[]{:S(2)}) %collective-permute-start.23) | collective-permute-done | bytes 32800 | tf_op jit(solution)/shard_map/ppermute | solution.py:192
  54.8 0.8 %collective-permute-done.22 = f32[128,128]{1,0:T(8,128)S(1)} collective-permute-done((f32[128,128]{1,0:T(8,128)S(1)}, f32[128,128]{1,0:T(8,128)S(1)}, u32[]{:S(2)}, u32[]{:S(2)}) %collective-permute-start.22) | collective-permute-done | bytes 65568 | tf_op jit(solution)/shard_map/ppermute | solution.py:192
  55.6 0.6 %fusion.2 = (f32[128,64]{0,1:T(8,128)}, f32[128,64]{0,1:T(8,128)}) fusion(f32[128,128]{1,0:T(8,128)S(1)} %collective-permute-done.22, f32[64,128]{1,0:T(8,128)S(1)} %collective-permute-done.23, f32[96,128]{1,0:T(8,128)S(1)} %collective-permute-done.20, f32[128,128]{1,0:T(8,128)S(1)} %join.5), kind=kLoop, calls=%fused_computation.3 | loop fusion | flops 49152 | bytes 262144 | tf_op jit(solution)/shard_map/transpose | solution.py:291
  (27 shorter events, 0.2 us)
Async XLA Ops:
  3.4 8.0 %collective-permute-start = (f32[112,128]{1,0:T(8,128)S(1)}, f32[112,128]{1,0:T(8,128)S(1)}, u32[]{:S(2)}, u32[]{:S(2)}) collective-permute-start(f32[112,128]{1,0:T(8,128)S(1)} %get-tuple-element.16.refs_0_), channel_id=1, source_target_pairs={{0,1},{1,0},{2,3},{3,2},{4,5},{5,4},{6,7},{7,6},{8,9},{9,8},{10,11... | collective-permute-start | bytes 172040 | tf_op jit(solution)/shard_map/ppermute | solution.py:192
  6.5 6.2 %collective-permute-start.1 = (f32[112,128]{1,0:T(8,128)S(1)}, f32[112,128]{1,0:T(8,128)S(1)}, u32[]{:S(2)}, u32[]{:S(2)}) collective-permute-start(f32[112,128]{1,0:T(8,128)S(1)} %get-tuple-element.16.refs_0_), channel_id=1, source_target_pairs={{0,2},{1,3},{2,0},{3,1},{4,6},{5,7},{6,4},{7,5},{8,10},{9,11},{10,... | collective-permute-start | bytes 172040 | tf_op jit(solution)/shard_map/ppermute | solution.py:192
  9.2 6.0 %collective-permute-start.2 = (f32[112,128]{1,0:T(8,128)S(1)}, f32[112,128]{1,0:T(8,128)S(1)}, u32[]{:S(2)}, u32[]{:S(2)}) collective-permute-start(f32[112,128]{1,0:T(8,128)S(1)} %get-tuple-element.16.refs_0_), channel_id=1, source_target_pairs={{0,3},{1,2},{2,1},{3,0},{4,7},{5,6},{6,5},{7,4},{8,11},{9,10},{10,... | collective-permute-start | bytes 172040 | tf_op jit(solution)/shard_map/ppermute | solution.py:192
  10.2 1.3 %collective-permute-start.3 = (f32[64,128]{1,0:T(8,128)S(1)}, f32[64,128]{1,0:T(8,128)S(1)}, u32[]{:S(2)}, u32[]{:S(2)}) collective-permute-start(f32[64,128]{1,0:T(8,128)S(1)} %time_part.3), channel_id=1, source_target_pairs={{0,8},{1,9},{2,10},{3,11},{4,12},{5,13},{6,14},{7,15},{8,0},{9,1},... | collective-permute-start | bytes 98312 | tf_op jit(solution)/shard_map/ppermute | solution.py:192
  15.3 4.4 %collective-permute-start.4 = (f32[96,128]{1,0:T(8,128)S(1)}, f32[96,128]{1,0:T(8,128)S(1)}, u32[]{:S(2)}, u32[]{:S(2)}) collective-permute-start(f32[96,128]{1,0:T(8,128)S(1)} %get-tuple-element.19), channel_id=1, source_target_pairs={{0,4},{1,5},{2,6},{3,7},{4,0},{5,1},{6,2},{7,3},{8,12},{9,13},{10,... | collective-permute-start | bytes 147464 | tf_op jit(solution)/shard_map/ppermute | solution.py:192
  16.9 1.4 %collective-permute-start.5 = (f32[80,128]{1,0:T(8,128)S(1)}, f32[80,128]{1,0:T(8,128)S(1)}, u32[]{:S(2)}, u32[]{:S(2)}) collective-permute-start(f32[80,128]{1,0:T(8,128)S(1)} %get-tuple-element.20.own), channel_id=1, source_target_pairs={{0,8},{1,9},{2,10},{3,11},{4,12},{5,13},{6,14},{7,15},{8,0},{9,1},... | collective-permute-start | bytes 122888 | tf_op jit(solution)/shard_map/ppermute | solution.py:192
  16.9 4.8 %collective-permute-start.7 = (f32[64,128]{1,0:T(8,128)S(1)}, f32[64,128]{1,0:T(8,128)S(1)}, u32[]{:S(2)}, u32[]{:S(2)}) collective-permute-start(f32[64,128]{1,0:T(8,128)S(1)} %add.54.refs_4_.time_part), channel_id=1, source_target_pairs={{0,20},{1,21},{2,22},{3,23},{4,16},{5,17},{6,18},{7,19},{8,28},{9,... | collective-permute-start | bytes 98312 | tf_op jit(solution)/shard_map/ppermute | solution.py:192
  18.3 4.3 %collective-permute-start.6 = (f32[128,128]{1,0:T(8,128)S(1)}, f32[128,128]{1,0:T(8,128)S(1)}, u32[]{:S(2)}, u32[]{:S(2)}) collective-permute-start(f32[128,128]{1,0:T(8,128)S(1)} %join.3), channel_id=1, source_target_pairs={{0,16},{1,17},{2,18},{3,19},{4,20},{5,21},{6,22},{7,23},{8,24},{9,... | collective-permute-start | bytes 196616 | tf_op jit(solution)/shard_map/ppermute | solution.py:192
  24.0 6.8 %collective-permute-start.10 = (f32[112,128]{1,0:T(8,128)S(1)}, f32[112,128]{1,0:T(8,128)S(1)}, u32[]{:S(2)}, u32[]{:S(2)}) collective-permute-start(f32[112,128]{1,0:T(8,128)S(1)} %src_dst_part.2.refs_0_), channel_id=1, source_target_pairs={{0,3},{1,2},{2,1},{3,0},{4,7},{5,6},{6,5},{7,4},{8,11},{9,10},{10,... | collective-permute-start | bytes 172040 | tf_op jit(solution)/shard_map/ppermute | solution.py:192
  25.3 5.5 %collective-permute-start.8 = (f32[112,128]{1,0:T(8,128)S(1)}, f32[112,128]{1,0:T(8,128)S(1)}, u32[]{:S(2)}, u32[]{:S(2)}) collective-permute-start(f32[112,128]{1,0:T(8,128)S(1)} %src_dst_part.2.refs_0_), channel_id=1, source_target_pairs={{0,1},{1,0},{2,3},{3,2},{4,5},{5,4},{6,7},{7,6},{8,9},{9,8},{10,11... | collective-permute-start | bytes 172040 | tf_op jit(solution)/shard_map/ppermute | solution.py:192
  25.6 5.2 %collective-permute-start.9 = (f32[112,128]{1,0:T(8,128)S(1)}, f32[112,128]{1,0:T(8,128)S(1)}, u32[]{:S(2)}, u32[]{:S(2)}) collective-permute-start(f32[112,128]{1,0:T(8,128)S(1)} %src_dst_part.2.refs_0_), channel_id=1, source_target_pairs={{0,2},{1,3},{2,0},{3,1},{4,6},{5,7},{6,4},{7,5},{8,10},{9,11},{10,... | collective-permute-start | bytes 172040 | tf_op jit(solution)/shard_map/ppermute | solution.py:192
  29.5 1.3 %collective-permute-start.11 = (f32[64,128]{1,0:T(8,128)S(1)}, f32[64,128]{1,0:T(8,128)S(1)}, u32[]{:S(2)}, u32[]{:S(2)}) collective-permute-start(f32[64,128]{1,0:T(8,128)S(1)} %time_part.4), channel_id=1, source_target_pairs={{0,8},{1,9},{2,10},{3,11},{4,12},{5,13},{6,14},{7,15},{8,0},{9,1},... | collective-permute-start | bytes 98312 | tf_op jit(solution)/shard_map/ppermute | solution.py:192
  31.0 4.2 %collective-permute-start.12 = (f32[96,128]{1,0:T(8,128)S(1)}, f32[96,128]{1,0:T(8,128)S(1)}, u32[]{:S(2)}, u32[]{:S(2)}) collective-permute-start(f32[96,128]{1,0:T(8,128)S(1)} %get-tuple-element.21), channel_id=1, source_target_pairs={{0,4},{1,5},{2,6},{3,7},{4,0},{5,1},{6,2},{7,3},{8,12},{9,13},{10,... | collective-permute-start | bytes 147464 | tf_op jit(solution)/shard_map/ppermute | solution.py:192
  32.6 1.3 %collective-permute-start.13 = (f32[80,128]{1,0:T(8,128)S(1)}, f32[80,128]{1,0:T(8,128)S(1)}, u32[]{:S(2)}, u32[]{:S(2)}) collective-permute-start(f32[80,128]{1,0:T(8,128)S(1)} %get-tuple-element.22.own), channel_id=1, source_target_pairs={{0,8},{1,9},{2,10},{3,11},{4,12},{5,13},{6,14},{7,15},{8,0},{9,1},... | collective-permute-start | bytes 122888 | tf_op jit(solution)/shard_map/ppermute | solution.py:192
  32.6 4.8 %collective-permute-start.15 = (f32[64,128]{1,0:T(8,128)S(1)}, f32[64,128]{1,0:T(8,128)S(1)}, u32[]{:S(2)}, u32[]{:S(2)}) collective-permute-start(f32[64,128]{1,0:T(8,128)S(1)} %add.60.refs_4_.time_part), channel_id=1, source_target_pairs={{0,20},{1,21},{2,22},{3,23},{4,16},{5,17},{6,18},{7,19},{8,28},{9,... | collective-permute-start | bytes 98312 | tf_op jit(solution)/shard_map/ppermute | solution.py:192
  33.9 4.3 %collective-permute-start.14 = (f32[128,128]{1,0:T(8,128)S(1)}, f32[128,128]{1,0:T(8,128)S(1)}, u32[]{:S(2)}, u32[]{:S(2)}) collective-permute-start(f32[128,128]{1,0:T(8,128)S(1)} %join.4), channel_id=1, source_target_pairs={{0,16},{1,17},{2,18},{3,19},{4,20},{5,21},{6,22},{7,23},{8,24},{9,... | collective-permute-start | bytes 196616 | tf_op jit(solution)/shard_map/ppermute | solution.py:192
  39.6 6.8 %collective-permute-start.16 = (f32[112,128]{1,0:T(8,128)S(1)}, f32[112,128]{1,0:T(8,128)S(1)}, u32[]{:S(2)}, u32[]{:S(2)}) collective-permute-start(f32[112,128]{1,0:T(8,128)S(1)} %src_dst_part.3.refs_0_), channel_id=1, source_target_pairs={{0,1},{1,0},{2,3},{3,2},{4,5},{5,4},{6,7},{7,6},{8,9},{9,8},{10,11... | collective-permute-start | bytes 172040 | tf_op jit(solution)/shard_map/ppermute | solution.py:192
  41.3 6.4 %collective-permute-start.17 = (f32[112,128]{1,0:T(8,128)S(1)}, f32[112,128]{1,0:T(8,128)S(1)}, u32[]{:S(2)}, u32[]{:S(2)}) collective-permute-start(f32[112,128]{1,0:T(8,128)S(1)} %src_dst_part.3.refs_0_), channel_id=1, source_target_pairs={{0,2},{1,3},{2,0},{3,1},{4,6},{5,7},{6,4},{7,5},{8,10},{9,11},{10,... | collective-permute-start | bytes 172040 | tf_op jit(solution)/shard_map/ppermute | solution.py:192
  42.5 6.1 %collective-permute-start.18 = (f32[112,128]{1,0:T(8,128)S(1)}, f32[112,128]{1,0:T(8,128)S(1)}, u32[]{:S(2)}, u32[]{:S(2)}) collective-permute-start(f32[112,128]{1,0:T(8,128)S(1)} %src_dst_part.3.refs_0_), channel_id=1, source_target_pairs={{0,3},{1,2},{2,1},{3,0},{4,7},{5,6},{6,5},{7,4},{8,11},{9,10},{10,... | collective-permute-start | bytes 172040 | tf_op jit(solution)/shard_map/ppermute | solution.py:192
  45.1 1.3 %collective-permute-start.19 = (f32[64,128]{1,0:T(8,128)S(1)}, f32[64,128]{1,0:T(8,128)S(1)}, u32[]{:S(2)}, u32[]{:S(2)}) collective-permute-start(f32[64,128]{1,0:T(8,128)S(1)} %time_part.5), channel_id=1, source_target_pairs={{0,8},{1,9},{2,10},{3,11},{4,12},{5,13},{6,14},{7,15},{8,0},{9,1},... | collective-permute-start | bytes 98312 | tf_op jit(solution)/shard_map/ppermute | solution.py:192
  48.8 4.2 %collective-permute-start.20 = (f32[96,128]{1,0:T(8,128)S(1)}, f32[96,128]{1,0:T(8,128)S(1)}, u32[]{:S(2)}, u32[]{:S(2)}) collective-permute-start(f32[96,128]{1,0:T(8,128)S(1)} %get-tuple-element.23), channel_id=1, source_target_pairs={{0,4},{1,5},{2,6},{3,7},{4,0},{5,1},{6,2},{7,3},{8,12},{9,13},{10,... | collective-permute-start | bytes 147464 | tf_op jit(solution)/shard_map/ppermute | solution.py:192
  50.0 1.3 %collective-permute-start.21 = (f32[80,128]{1,0:T(8,128)S(1)}, f32[80,128]{1,0:T(8,128)S(1)}, u32[]{:S(2)}, u32[]{:S(2)}) collective-permute-start(f32[80,128]{1,0:T(8,128)S(1)} %get-tuple-element.24.own), channel_id=1, source_target_pairs={{0,8},{1,9},{2,10},{3,11},{4,12},{5,13},{6,14},{7,15},{8,0},{9,1},... | collective-permute-start | bytes 122888 | tf_op jit(solution)/shard_map/ppermute | solution.py:192
  50.0 4.8 %collective-permute-start.23 = (f32[64,128]{1,0:T(8,128)S(1)}, f32[64,128]{1,0:T(8,128)S(1)}, u32[]{:S(2)}, u32[]{:S(2)}) collective-permute-start(f32[64,128]{1,0:T(8,128)S(1)} %add.66.refs_4_.time_part), channel_id=1, source_target_pairs={{0,20},{1,21},{2,22},{3,23},{4,16},{5,17},{6,18},{7,19},{8,28},{9,... | collective-permute-start | bytes 98312 | tf_op jit(solution)/shard_map/ppermute | solution.py:192
  51.3 4.3 %collective-permute-start.22 = (f32[128,128]{1,0:T(8,128)S(1)}, f32[128,128]{1,0:T(8,128)S(1)}, u32[]{:S(2)}, u32[]{:S(2)}) collective-permute-start(f32[128,128]{1,0:T(8,128)S(1)} %join.5), channel_id=1, source_target_pairs={{0,16},{1,17},{2,18},{3,19},{4,20},{5,21},{6,22},{7,23},{8,24},{9,... | collective-permute-start | bytes 196616 | tf_op jit(solution)/shard_map/ppermute | solution.py:192

commit v2 on v1

--- a/solution.py
+++ b/solution.py
@@ -14,7 +14,6 @@
 hour_weight = 32.0
 day_weight = 64.0
 step_rate = 0.1
-highest = lax.Precision.HIGHEST
 f32 = jnp.float32
 bf16 = jnp.bfloat16
 LANES = 128
@@ -24,18 +23,26 @@
 PARAMS = pltpu.CompilerParams(vmem_limit_bytes=24 << 20)
 
 
+def split(x):
+    high = x.astype(bf16)
+    return high, (x - high.astype(f32)).astype(bf16)
+
+
 def halves(x):
-    high = x.astype(bf16)
-    low = (x - high.astype(f32)).astype(bf16)
-    return jnp.concatenate([high, low], 0)
+    return jnp.concatenate(split(x), 0)
 
 
 def gram(x):
-    return lax.dot_general(x, x, BY_LANES, precision=highest, preferred_element_type=f32)
+    high, low = split(x)
+    left, right = jnp.concatenate([high, high, low], 1), jnp.concatenate([high, low, high], 1)
+    return lax.dot_general(left, right, BY_LANES, preferred_element_type=f32)
 
 
 def times(a, b):
-    return jnp.dot(a, b, precision=highest, preferred_element_type=f32)
+    (a_high, a_low), (b_high, b_low) = split(a), split(b)
+    product = jnp.dot(a_high, b_high, preferred_element_type=f32)
+    product = product + jnp.dot(a_high, b_low, preferred_element_type=f32)
+    return product + jnp.dot(a_low, b_high, preferred_element_type=f32)
 
 
 def packed(x):
@@ -260,8 +267,9 @@
         for mask in range(1, tm_size):
             others.append(exchanged(mixed, 0, 0, mask))
         time_part = second_kernel(traffic, src_now, dst_now, time_now)
+        add_time = exchanged(time_part, 2, 1, 0)
         time_part = time_part + exchanged(time_part, 1, 0, 0)
-        add_time = exchanged(time_part, 2, 1, 0)
+        add_time = add_time + exchanged(add_time, 1, 0, 0)
         src_time, dst_smooth = third_kernel(mixed, *others, time_part)
         other_smooth = exchanged(dst_smooth, 1, 0, 0)
         dst_time = join(dst_smooth, other_smooth, time_part)

time: 56.4 us -> 66.9 us (1.19)
  waiting for transfers between devices: 17.8 us -> 27.9 us
  starting transfers between devices: 26.9 us -> 27.7 us
    ppermute x24 -> x27, waiting for transfers between devices: 17.8 us -> 27.9 us  [exchanged(): return lax.ppermute(x, AXES, route)]
    ppermute x24 -> x27, starting transfers between devices: 26.9 us -> 27.7 us  [exchanged(): return lax.ppermute(x, AXES, route)]
  transfers between devices with their start and end apart: 24 -> 27, of which waited for: 14 -> 15; matrix products, arithmetic and copies ran while one was open for 2% -> 1% of each run, Pallas kernels for 6% -> 5%
where the time goes in v2:
time: 66.9 us; the launch traced here: 66.8 us
  waiting for transfers between devices  27.9 us (42%)
  starting transfers between devices  27.7 us (41%)
  Pallas kernels  8.81 us (13%)
  other arithmetic  1.36 us (2%)
  between operations  0.8 us (1%)
    ppermute x27, waiting for transfers between devices, exchanged(): return lax.ppermute(x, AXES, route)  27.9 us
    ppermute x27, starting transfers between devices, exchanged(): return lax.ppermute(x, AXES, route)  27.7 us
    pallas_call x3, Pallas kernels, on_device(): time_part = second_kernel(traffic, src_now, dst_now, time_now)  3 us
    pallas_call x1, Pallas kernels, on_device(): mixed, traffic, src_now, dst_now, time_now = zero_kernel(*given)  2.71 us
    pallas_call x2, Pallas kernels, on_device(): mixed = first_kernel(traffic, src_now, dst_now, time_now)  2.53 us
  transfers between devices with their start and end apart: 27, of which 15 were waited for; matrix products, arithmetic and copies ran while one was open for 1% of the time, Pallas kernels for 5%

profile of v2, /device:TPU:0, one launch (start us, length us, event | category | flops | bytes accessed | tf_op | source)
XLA Modules:
  0.0 66.8 jit_solution(17240035565098657404)
XLA Ops:
  0.6 2.7 %entry.1 = (f32[112,128]{1,0:T(8,128)S(1)}, bf16[64,128,128]{2,1,0:T(8,128)(2,1)S(1)}, f32[64,64]{1,0:T(8,128)S(1)}, f32[64,128]{1,0:T(8,128)S(1)}, f32[64,128]{1,0:T(8,128)S(1)}) custom-call(bf16[64,128,128]{2,1,0:T(8,128)(2,1)} %traffic_in.1, f32[64,64]{1,0:T(8,128)} %src_in.1, f32[64,128]{1,0:T(8,128)} %bitcast.6, f32[64,128]{1,0:T(8,128)} %bitcast.7), custom_call_target="tpu_custom_call" | custom-call | tf_op jit(solution)/shard_map/entry/pallas_call | solution.py:263
  3.3 3.1 %collective-permute-start = (f32[112,128]{1,0:T(8,128)S(1)}, f32[112,128]{1,0:T(8,128)S(1)}, u32[]{:S(2)}, u32[]{:S(2)}) collective-permute-start(f32[112,128]{1,0:T(8,128)S(1)} %get-tuple-element.16.refs_0_), channel_id=1, source_target_pairs={{0,1},{1,0},{2,3},{3,2},{4,5},{5,4},{6,7},{7,6},{8,9},{9,8},{10,11... | collective-permute-start | bytes 172040 | tf_op jit(solution)/shard_map/ppermute | solution.py:199
  6.5 2.6 %collective-permute-start.1 = (f32[112,128]{1,0:T(8,128)S(1)}, f32[112,128]{1,0:T(8,128)S(1)}, u32[]{:S(2)}, u32[]{:S(2)}) collective-permute-start(f32[112,128]{1,0:T(8,128)S(1)} %get-tuple-element.16.refs_0_), channel_id=1, source_target_pairs={{0,2},{1,3},{2,0},{3,1},{4,6},{5,7},{6,4},{7,5},{8,10},{9,11},{10,... | collective-permute-start | bytes 172040 | tf_op jit(solution)/shard_map/ppermute | solution.py:199
  9.1 1.0 %time_part.3 = f32[64,128]{1,0:T(8,128)S(1)} custom-call(bf16[64,128,128]{2,1,0:T(8,128)(2,1)S(1)} %get-tuple-element.14.traffic, f32[64,64]{1,0:T(8,128)S(1)} %get-tuple-element.15.src, f32[64,128]{1,0:T(8,128)S(1)} %get-tuple-element.17.dst, f32[64,128]{1,0:T(8,128)S(1)} %get-tuple-element.18.time), custom_call_target="tpu_custom_call" | custom-call | tf_op jit(solution)/shard_map/time_part/pallas_call | solution.py:269
  10.1 0.1 collective-permute-start.3
  10.2 1.2 %collective-permute-done.3 = f32[64,128]{1,0:T(8,128)S(1)} collective-permute-done((f32[64,128]{1,0:T(8,128)S(1)}, f32[64,128]{1,0:T(8,128)S(1)}, u32[]{:S(2)}, u32[]{:S(2)}) %collective-permute-start.3) | collective-permute-done | bytes 32800 | tf_op jit(solution)/shard_map/ppermute | solution.py:199
  11.4 1.3 %collective-permute-done.1.refs_2_ = f32[112,128]{1,0:T(8,128)S(1)} collective-permute-done((f32[112,128]{1,0:T(8,128)S(1)}, f32[112,128]{1,0:T(8,128)S(1)}, u32[]{:S(2)}, u32[]{:S(2)}) %collective-permute-start.1) | collective-permute-done | bytes 57376 | tf_op jit(solution)/shard_map/ppermute | solution.py:199
  12.7 2.4 %collective-permute-done.2.refs_3_ = f32[112,128]{1,0:T(8,128)S(1)} collective-permute-done((f32[112,128]{1,0:T(8,128)S(1)}, f32[112,128]{1,0:T(8,128)S(1)}, u32[]{:S(2)}, u32[]{:S(2)}) %collective-permute-start.2) | collective-permute-done | bytes 57376 | tf_op jit(solution)/shard_map/ppermute | solution.py:199
  15.1 0.2 tm_sums.3
  15.2 1.6 %collective-permute-start.4 = (f32[96,128]{1,0:T(8,128)S(1)}, f32[96,128]{1,0:T(8,128)S(1)}, u32[]{:S(2)}, u32[]{:S(2)}) collective-permute-start(f32[96,128]{1,0:T(8,128)S(1)} %get-tuple-element.19), channel_id=1, source_target_pairs={{0,4},{1,5},{2,6},{3,7},{4,0},{5,1},{6,2},{7,3},{8,12},{9,13},{10,... | collective-permute-start | bytes 147464 | tf_op jit(solution)/shard_map/ppermute | solution.py:199
  16.8 1.4 %collective-permute-start.7 = (f32[64,128]{1,0:T(8,128)S(1)}, f32[64,128]{1,0:T(8,128)S(1)}, u32[]{:S(2)}, u32[]{:S(2)}) collective-permute-start(f32[64,128]{1,0:T(8,128)S(1)} %time_part.3), channel_id=1, source_target_pairs={{0,20},{1,21},{2,22},{3,23},{4,16},{5,17},{6,18},{7,19},{8,28},{9,... | collective-permute-start | bytes 98312 | tf_op jit(solution)/shard_map/ppermute | solution.py:199
  18.2 3.4 %collective-permute-done.7 = f32[64,128]{1,0:T(8,128)S(1)} collective-permute-done((f32[64,128]{1,0:T(8,128)S(1)}, f32[64,128]{1,0:T(8,128)S(1)}, u32[]{:S(2)}, u32[]{:S(2)}) %collective-permute-start.7) | collective-permute-done | bytes 32800 | tf_op jit(solution)/shard_map/ppermute | solution.py:199
  21.6 1.6 %collective-permute-start.6 = (f32[128,128]{1,0:T(8,128)S(1)}, f32[128,128]{1,0:T(8,128)S(1)}, u32[]{:S(2)}, u32[]{:S(2)}) collective-permute-start(f32[128,128]{1,0:T(8,128)S(1)} %join.3), channel_id=1, source_target_pairs={{0,16},{1,17},{2,18},{3,19},{4,20},{5,21},{6,22},{7,23},{8,24},{9,... | collective-permute-start | bytes 196616 | tf_op jit(solution)/shard_map/ppermute | solution.py:199
  23.2 0.1 fusion.19
  23.3 2.9 %collective-permute-done.6 = f32[128,128]{1,0:T(8,128)S(1)} collective-permute-done((f32[128,128]{1,0:T(8,128)S(1)}, f32[128,128]{1,0:T(8,128)S(1)}, u32[]{:S(2)}, u32[]{:S(2)}) %collective-permute-start.6) | collective-permute-done | bytes 65568 | tf_op jit(solution)/shard_map/ppermute | solution.py:199
  26.2 1.3 %src_dst_part.2.refs_0_ = f32[112,128]{1,0:T(8,128)S(1)} custom-call(bf16[64,128,128]{2,1,0:T(8,128)(2,1)S(1)} %get-tuple-element.14.traffic, f32[64,64]{1,0:T(8,128)S(1)} %fusion.15.src, f32[64,128]{1,0:T(8,128)S(1)} %get-tuple-element.30.dst, f32[64,128]{1,0:T(8,128)S(1)} %get-tuple-element.29.time), custom_call_target="tpu_custom_call" | custom-call | tf_op jit(solution)/shard_map/src_dst_part/pallas_call | solution.py:265
  27.5 1.1 %collective-permute-start.10 = (f32[112,128]{1,0:T(8,128)S(1)}, f32[112,128]{1,0:T(8,128)S(1)}, u32[]{:S(2)}, u32[]{:S(2)}) collective-permute-start(f32[112,128]{1,0:T(8,128)S(1)} %src_dst_part.2.refs_0_), channel_id=1, source_target_pairs={{0,2},{1,3},{2,0},{3,1},{4,6},{5,7},{6,4},{7,5},{8,10},{9,11},{10,... | collective-permute-start | bytes 172040 | tf_op jit(solution)/shard_map/ppermute | solution.py:199
  28.6 0.8 %collective-permute-start.11 = (f32[112,128]{1,0:T(8,128)S(1)}, f32[112,128]{1,0:T(8,128)S(1)}, u32[]{:S(2)}, u32[]{:S(2)}) collective-permute-start(f32[112,128]{1,0:T(8,128)S(1)} %src_dst_part.2.refs_0_), channel_id=1, source_target_pairs={{0,3},{1,2},{2,1},{3,0},{4,7},{5,6},{6,5},{7,4},{8,11},{9,10},{10,... | collective-permute-start | bytes 172040 | tf_op jit(solution)/shard_map/ppermute | solution.py:199
  29.4 1.7 %collective-permute-start.9 = (f32[112,128]{1,0:T(8,128)S(1)}, f32[112,128]{1,0:T(8,128)S(1)}, u32[]{:S(2)}, u32[]{:S(2)}) collective-permute-start(f32[112,128]{1,0:T(8,128)S(1)} %src_dst_part.2.refs_0_), channel_id=1, source_target_pairs={{0,1},{1,0},{2,3},{3,2},{4,5},{5,4},{6,7},{7,6},{8,9},{9,8},{10,11... | collective-permute-start | bytes 172040 | tf_op jit(solution)/shard_map/ppermute | solution.py:199
  31.1 1.0 %time_part.4 = f32[64,128]{1,0:T(8,128)S(1)} custom-call(bf16[64,128,128]{2,1,0:T(8,128)(2,1)S(1)} %get-tuple-element.14.traffic, f32[64,64]{1,0:T(8,128)S(1)} %fusion.15.src, f32[64,128]{1,0:T(8,128)S(1)} %get-tuple-element.30.dst, f32[64,128]{1,0:T(8,128)S(1)} %get-tuple-element.29.time), custom_call_target="tpu_custom_call" | custom-call | tf_op jit(solution)/shard_map/time_part/pallas_call | solution.py:269
  32.1 0.1 collective-permute-start.12
  32.2 1.2 %collective-permute-done.12 = f32[64,128]{1,0:T(8,128)S(1)} collective-permute-done((f32[64,128]{1,0:T(8,128)S(1)}, f32[64,128]{1,0:T(8,128)S(1)}, u32[]{:S(2)}, u32[]{:S(2)}) %collective-permute-start.12) | collective-permute-done | bytes 32800 | tf_op jit(solution)/shard_map/ppermute | solution.py:199
  33.4 0.4 collective-permute-done.10.refs_2_
  33.8 0.9 %collective-permute-done.11.refs_3_ = f32[112,128]{1,0:T(8,128)S(1)} collective-permute-done((f32[112,128]{1,0:T(8,128)S(1)}, f32[112,128]{1,0:T(8,128)S(1)}, u32[]{:S(2)}, u32[]{:S(2)}) %collective-permute-start.11) | collective-permute-done | bytes 57376 | tf_op jit(solution)/shard_map/ppermute | solution.py:199
  34.7 0.2 tm_sums.4
  34.9 0.6 collective-permute-start.13
  35.5 2.5 %collective-permute-start.16 = (f32[64,128]{1,0:T(8,128)S(1)}, f32[64,128]{1,0:T(8,128)S(1)}, u32[]{:S(2)}, u32[]{:S(2)}) collective-permute-start(f32[64,128]{1,0:T(8,128)S(1)} %time_part.4), channel_id=1, source_target_pairs={{0,20},{1,21},{2,22},{3,23},{4,16},{5,17},{6,18},{7,19},{8,28},{9,... | collective-permute-start | bytes 98312 | tf_op jit(solution)/shard_map/ppermute | solution.py:199
  37.9 2.4 %collective-permute-done.16 = f32[64,128]{1,0:T(8,128)S(1)} collective-permute-done((f32[64,128]{1,0:T(8,128)S(1)}, f32[64,128]{1,0:T(8,128)S(1)}, u32[]{:S(2)}, u32[]{:S(2)}) %collective-permute-start.16) | collective-permute-done | bytes 32800 | tf_op jit(solution)/shard_map/ppermute | solution.py:199
  40.3 1.5 %collective-permute-start.15 = (f32[128,128]{1,0:T(8,128)S(1)}, f32[128,128]{1,0:T(8,128)S(1)}, u32[]{:S(2)}, u32[]{:S(2)}) collective-permute-start(f32[128,128]{1,0:T(8,128)S(1)} %join.4), channel_id=1, source_target_pairs={{0,16},{1,17},{2,18},{3,19},{4,20},{5,21},{6,22},{7,23},{8,24},{9,... | collective-permute-start | bytes 196616 | tf_op jit(solution)/shard_map/ppermute | solution.py:199
  41.9 0.1 fusion.18
  42.0 2.9 %collective-permute-done.15 = f32[128,128]{1,0:T(8,128)S(1)} collective-permute-done((f32[128,128]{1,0:T(8,128)S(1)}, f32[128,128]{1,0:T(8,128)S(1)}, u32[]{:S(2)}, u32[]{:S(2)}) %collective-permute-start.15) | collective-permute-done | bytes 65568 | tf_op jit(solution)/shard_map/ppermute | solution.py:199
  44.9 1.3 %src_dst_part.3.refs_0_ = f32[112,128]{1,0:T(8,128)S(1)} custom-call(bf16[64,128,128]{2,1,0:T(8,128)(2,1)S(1)} %get-tuple-element.14.traffic, f32[64,64]{1,0:T(8,128)S(1)} %fusion.16.src, f32[64,128]{1,0:T(8,128)S(1)} %get-tuple-element.28.dst, f32[64,128]{1,0:T(8,128)S(1)} %get-tuple-element.27.time), custom_call_target="tpu_custom_call" | custom-call | tf_op jit(solution)/shard_map/src_dst_part/pallas_call | solution.py:265
  46.2 1.0 %collective-permute-start.18 = (f32[112,128]{1,0:T(8,128)S(1)}, f32[112,128]{1,0:T(8,128)S(1)}, u32[]{:S(2)}, u32[]{:S(2)}) collective-permute-start(f32[112,128]{1,0:T(8,128)S(1)} %src_dst_part.3.refs_0_), channel_id=1, source_target_pairs={{0,1},{1,0},{2,3},{3,2},{4,5},{5,4},{6,7},{7,6},{8,9},{9,8},{10,11... | collective-permute-start | bytes 172040 | tf_op jit(solution)/shard_map/ppermute | solution.py:199
  47.1 1.7 %collective-permute-start.19 = (f32[112,128]{1,0:T(8,128)S(1)}, f32[112,128]{1,0:T(8,128)S(1)}, u32[]{:S(2)}, u32[]{:S(2)}) collective-permute-start(f32[112,128]{1,0:T(8,128)S(1)} %src_dst_part.3.refs_0_), channel_id=1, source_target_pairs={{0,2},{1,3},{2,0},{3,1},{4,6},{5,7},{6,4},{7,5},{8,10},{9,11},{10,... | collective-permute-start | bytes 172040 | tf_op jit(solution)/shard_map/ppermute | solution.py:199
  48.8 1.8 %collective-permute-start.20 = (f32[112,128]{1,0:T(8,128)S(1)}, f32[112,128]{1,0:T(8,128)S(1)}, u32[]{:S(2)}, u32[]{:S(2)}) collective-permute-start(f32[112,128]{1,0:T(8,128)S(1)} %src_dst_part.3.refs_0_), channel_id=1, source_target_pairs={{0,3},{1,2},{2,1},{3,0},{4,7},{5,6},{6,5},{7,4},{8,11},{9,10},{10,... | collective-permute-start | bytes 172040 | tf_op jit(solution)/shard_map/ppermute | solution.py:199
  50.6 1.0 %time_part.5 = f32[64,128]{1,0:T(8,128)S(1)} custom-call(bf16[64,128,128]{2,1,0:T(8,128)(2,1)S(1)} %get-tuple-element.14.traffic, f32[64,64]{1,0:T(8,128)S(1)} %fusion.16.src, f32[64,128]{1,0:T(8,128)S(1)} %get-tuple-element.28.dst, f32[64,128]{1,0:T(8,128)S(1)} %get-tuple-element.27.time), custom_call_target="tpu_custom_call" | custom-call | tf_op jit(solution)/shard_map/time_part/pallas_call | solution.py:269
  51.7 1.2 %collective-permute-done.21 = f32[64,128]{1,0:T(8,128)S(1)} collective-permute-done((f32[64,128]{1,0:T(8,128)S(1)}, f32[64,128]{1,0:T(8,128)S(1)}, u32[]{:S(2)}, u32[]{:S(2)}) %collective-permute-start.21) | collective-permute-done | bytes 32800 | tf_op jit(solution)/shard_map/ppermute | solution.py:199
  52.9 0.8 %collective-permute-done.19.refs_2_ = f32[112,128]{1,0:T(8,128)S(1)} collective-permute-done((f32[112,128]{1,0:T(8,128)S(1)}, f32[112,128]{1,0:T(8,128)S(1)}, u32[]{:S(2)}, u32[]{:S(2)}) %collective-permute-start.19) | collective-permute-done | bytes 57376 | tf_op jit(solution)/shard_map/ppermute | solution.py:199
  53.7 1.2 %collective-permute-done.20.refs_3_ = f32[112,128]{1,0:T(8,128)S(1)} collective-permute-done((f32[112,128]{1,0:T(8,128)S(1)}, f32[112,128]{1,0:T(8,128)S(1)}, u32[]{:S(2)}, u32[]{:S(2)}) %collective-permute-start.20) | collective-permute-done | bytes 57376 | tf_op jit(solution)/shard_map/ppermute | solution.py:199
  54.9 0.2 tm_sums.5
  55.1 1.6 %collective-permute-start.22 = (f32[96,128]{1,0:T(8,128)S(1)}, f32[96,128]{1,0:T(8,128)S(1)}, u32[]{:S(2)}, u32[]{:S(2)}) collective-permute-start(f32[96,128]{1,0:T(8,128)S(1)} %get-tuple-element.23), channel_id=1, source_target_pairs={{0,4},{1,5},{2,6},{3,7},{4,0},{5,1},{6,2},{7,3},{8,12},{9,13},{10,... | collective-permute-start | bytes 147464 | tf_op jit(solution)/shard_map/ppermute | solution.py:199
  56.7 1.4 %collective-permute-start.25 = (f32[64,128]{1,0:T(8,128)S(1)}, f32[64,128]{1,0:T(8,128)S(1)}, u32[]{:S(2)}, u32[]{:S(2)}) collective-permute-start(f32[64,128]{1,0:T(8,128)S(1)} %time_part.5), channel_id=1, source_target_pairs={{0,20},{1,21},{2,22},{3,23},{4,16},{5,17},{6,18},{7,19},{8,28},{9,... | collective-permute-start | bytes 98312 | tf_op jit(solution)/shard_map/ppermute | solution.py:199
  58.1 3.4 %collective-permute-done.25 = f32[64,128]{1,0:T(8,128)S(1)} collective-permute-done((f32[64,128]{1,0:T(8,128)S(1)}, f32[64,128]{1,0:T(8,128)S(1)}, u32[]{:S(2)}, u32[]{:S(2)}) %collective-permute-start.25) | collective-permute-done | bytes 32800 | tf_op jit(solution)/shard_map/ppermute | solution.py:199
  61.5 1.5 %collective-permute-start.24 = (f32[128,128]{1,0:T(8,128)S(1)}, f32[128,128]{1,0:T(8,128)S(1)}, u32[]{:S(2)}, u32[]{:S(2)}) collective-permute-start(f32[128,128]{1,0:T(8,128)S(1)} %join.5), channel_id=1, source_target_pairs={{0,16},{1,17},{2,18},{3,19},{4,20},{5,21},{6,22},{7,23},{8,24},{9,... | collective-permute-start | bytes 196616 | tf_op jit(solution)/shard_map/ppermute | solution.py:199
  63.1 0.1 fusion.17
  63.2 0.6 maximum_multiply_fusion.2
  63.8 2.3 %collective-permute-done.24 = f32[128,128]{1,0:T(8,128)S(1)} collective-permute-done((f32[128,128]{1,0:T(8,128)S(1)}, f32[128,128]{1,0:T(8,128)S(1)}, u32[]{:S(2)}, u32[]{:S(2)}) %collective-permute-start.24) | collective-permute-done | bytes 65568 | tf_op jit(solution)/shard_map/ppermute | solution.py:199
  66.1 0.6 fusion.2
  (33 shorter events, 0.3 us)
Async XLA Ops:
  3.3 8.0 %collective-permute-start = (f32[112,128]{1,0:T(8,128)S(1)}, f32[112,128]{1,0:T(8,128)S(1)}, u32[]{:S(2)}, u32[]{:S(2)}) collective-permute-start(f32[112,128]{1,0:T(8,128)S(1)} %get-tuple-element.16.refs_0_), channel_id=1, source_target_pairs={{0,1},{1,0},{2,3},{3,2},{4,5},{5,4},{6,7},{7,6},{8,9},{9,8},{10,11... | collective-permute-start | bytes 172040 | tf_op jit(solution)/shard_map/ppermute | solution.py:199
  6.5 6.2 %collective-permute-start.1 = (f32[112,128]{1,0:T(8,128)S(1)}, f32[112,128]{1,0:T(8,128)S(1)}, u32[]{:S(2)}, u32[]{:S(2)}) collective-permute-start(f32[112,128]{1,0:T(8,128)S(1)} %get-tuple-element.16.refs_0_), channel_id=1, source_target_pairs={{0,2},{1,3},{2,0},{3,1},{4,6},{5,7},{6,4},{7,5},{8,10},{9,11},{10,... | collective-permute-start | bytes 172040 | tf_op jit(solution)/shard_map/ppermute | solution.py:199
  9.1 6.0 %collective-permute-start.2 = (f32[112,128]{1,0:T(8,128)S(1)}, f32[112,128]{1,0:T(8,128)S(1)}, u32[]{:S(2)}, u32[]{:S(2)}) collective-permute-start(f32[112,128]{1,0:T(8,128)S(1)} %get-tuple-element.16.refs_0_), channel_id=1, source_target_pairs={{0,3},{1,2},{2,1},{3,0},{4,7},{5,6},{6,5},{7,4},{8,11},{9,10},{10,... | collective-permute-start | bytes 172040 | tf_op jit(solution)/shard_map/ppermute | solution.py:199
  10.1 1.3 %collective-permute-start.3 = (f32[64,128]{1,0:T(8,128)S(1)}, f32[64,128]{1,0:T(8,128)S(1)}, u32[]{:S(2)}, u32[]{:S(2)}) collective-permute-start(f32[64,128]{1,0:T(8,128)S(1)} %time_part.3), channel_id=1, source_target_pairs={{0,8},{1,9},{2,10},{3,11},{4,12},{5,13},{6,14},{7,15},{8,0},{9,1},... | collective-permute-start | bytes 98312 | tf_op jit(solution)/shard_map/ppermute | solution.py:199
  15.2 8.0 %collective-permute-start.4 = (f32[96,128]{1,0:T(8,128)S(1)}, f32[96,128]{1,0:T(8,128)S(1)}, u32[]{:S(2)}, u32[]{:S(2)}) collective-permute-start(f32[96,128]{1,0:T(8,128)S(1)} %get-tuple-element.19), channel_id=1, source_target_pairs={{0,4},{1,5},{2,6},{3,7},{4,0},{5,1},{6,2},{7,3},{8,12},{9,13},{10,... | collective-permute-start | bytes 147464 | tf_op jit(solution)/shard_map/ppermute | solution.py:199
  16.8 4.8 %collective-permute-start.5 = (f32[80,128]{1,0:T(8,128)S(1)}, f32[80,128]{1,0:T(8,128)S(1)}, u32[]{:S(2)}, u32[]{:S(2)}) collective-permute-start(f32[80,128]{1,0:T(8,128)S(1)} %get-tuple-element.20.own), channel_id=1, source_target_pairs={{0,8},{1,9},{2,10},{3,11},{4,12},{5,13},{6,14},{7,15},{8,0},{9,1},... | collective-permute-start | bytes 122888 | tf_op jit(solution)/shard_map/ppermute | solution.py:199
  16.8 4.8 %collective-permute-start.7 = (f32[64,128]{1,0:T(8,128)S(1)}, f32[64,128]{1,0:T(8,128)S(1)}, u32[]{:S(2)}, u32[]{:S(2)}) collective-permute-start(f32[64,128]{1,0:T(8,128)S(1)} %time_part.3), channel_id=1, source_target_pairs={{0,20},{1,21},{2,22},{3,23},{4,16},{5,17},{6,18},{7,19},{8,28},{9,... | collective-permute-start | bytes 98312 | tf_op jit(solution)/shard_map/ppermute | solution.py:199
  21.6 1.7 %collective-permute-start.8 = (f32[64,128]{1,0:T(8,128)S(1)}, f32[64,128]{1,0:T(8,128)S(1)}, u32[]{:S(2)}, u32[]{:S(2)}) collective-permute-start(f32[64,128]{1,0:T(8,128)S(1)} %collective-permute-done.7), channel_id=1, source_target_pairs={{0,8},{1,9},{2,10},{3,11},{4,12},{5,13},{6,14},{7,15},{8,0},{9,1},... | collective-permute-start | bytes 98312 | tf_op jit(solution)/shard_map/ppermute | solution.py:199
  21.6 4.6 %collective-permute-start.6 = (f32[128,128]{1,0:T(8,128)S(1)}, f32[128,128]{1,0:T(8,128)S(1)}, u32[]{:S(2)}, u32[]{:S(2)}) collective-permute-start(f32[128,128]{1,0:T(8,128)S(1)} %join.3), channel_id=1, source_target_pairs={{0,16},{1,17},{2,18},{3,19},{4,20},{5,21},{6,22},{7,23},{8,24},{9,... | collective-permute-start | bytes 196616 | tf_op jit(solution)/shard_map/ppermute | solution.py:199
  27.5 6.3 %collective-permute-start.10 = (f32[112,128]{1,0:T(8,128)S(1)}, f32[112,128]{1,0:T(8,128)S(1)}, u32[]{:S(2)}, u32[]{:S(2)}) collective-permute-start(f32[112,128]{1,0:T(8,128)S(1)} %src_dst_part.2.refs_0_), channel_id=1, source_target_pairs={{0,2},{1,3},{2,0},{3,1},{4,6},{5,7},{6,4},{7,5},{8,10},{9,11},{10,... | collective-permute-start | bytes 172040 | tf_op jit(solution)/shard_map/ppermute | solution.py:199
  28.6 6.1 %collective-permute-start.11 = (f32[112,128]{1,0:T(8,128)S(1)}, f32[112,128]{1,0:T(8,128)S(1)}, u32[]{:S(2)}, u32[]{:S(2)}) collective-permute-start(f32[112,128]{1,0:T(8,128)S(1)} %src_dst_part.2.refs_0_), channel_id=1, source_target_pairs={{0,3},{1,2},{2,1},{3,0},{4,7},{5,6},{6,5},{7,4},{8,11},{9,10},{10,... | collective-permute-start | bytes 172040 | tf_op jit(solution)/shard_map/ppermute | solution.py:199
  29.4 5.3 %collective-permute-start.9 = (f32[112,128]{1,0:T(8,128)S(1)}, f32[112,128]{1,0:T(8,128)S(1)}, u32[]{:S(2)}, u32[]{:S(2)}) collective-permute-start(f32[112,128]{1,0:T(8,128)S(1)} %src_dst_part.2.refs_0_), channel_id=1, source_target_pairs={{0,1},{1,0},{2,3},{3,2},{4,5},{5,4},{6,7},{7,6},{8,9},{9,8},{10,11... | collective-permute-start | bytes 172040 | tf_op jit(solution)/shard_map/ppermute | solution.py:199
  32.1 1.3 %collective-permute-start.12 = (f32[64,128]{1,0:T(8,128)S(1)}, f32[64,128]{1,0:T(8,128)S(1)}, u32[]{:S(2)}, u32[]{:S(2)}) collective-permute-start(f32[64,128]{1,0:T(8,128)S(1)} %time_part.4), channel_id=1, source_target_pairs={{0,8},{1,9},{2,10},{3,11},{4,12},{5,13},{6,14},{7,15},{8,0},{9,1},... | collective-permute-start | bytes 98312 | tf_op jit(solution)/shard_map/ppermute | solution.py:199
  34.9 7.0 %collective-permute-start.13 = (f32[96,128]{1,0:T(8,128)S(1)}, f32[96,128]{1,0:T(8,128)S(1)}, u32[]{:S(2)}, u32[]{:S(2)}) collective-permute-start(f32[96,128]{1,0:T(8,128)S(1)} %get-tuple-element.21), channel_id=1, source_target_pairs={{0,4},{1,5},{2,6},{3,7},{4,0},{5,1},{6,2},{7,3},{8,12},{9,13},{10,... | collective-permute-start | bytes 147464 | tf_op jit(solution)/shard_map/ppermute | solution.py:199
  35.5 4.8 %collective-permute-start.14 = (f32[80,128]{1,0:T(8,128)S(1)}, f32[80,128]{1,0:T(8,128)S(1)}, u32[]{:S(2)}, u32[]{:S(2)}) collective-permute-start(f32[80,128]{1,0:T(8,128)S(1)} %get-tuple-element.22.own), channel_id=1, source_target_pairs={{0,8},{1,9},{2,10},{3,11},{4,12},{5,13},{6,14},{7,15},{8,0},{9,1},... | collective-permute-start | bytes 122888 | tf_op jit(solution)/shard_map/ppermute | solution.py:199
  35.5 4.8 %collective-permute-start.16 = (f32[64,128]{1,0:T(8,128)S(1)}, f32[64,128]{1,0:T(8,128)S(1)}, u32[]{:S(2)}, u32[]{:S(2)}) collective-permute-start(f32[64,128]{1,0:T(8,128)S(1)} %time_part.4), channel_id=1, source_target_pairs={{0,20},{1,21},{2,22},{3,23},{4,16},{5,17},{6,18},{7,19},{8,28},{9,... | collective-permute-start | bytes 98312 | tf_op jit(solution)/shard_map/ppermute | solution.py:199
  40.3 1.7 %collective-permute-start.17 = (f32[64,128]{1,0:T(8,128)S(1)}, f32[64,128]{1,0:T(8,128)S(1)}, u32[]{:S(2)}, u32[]{:S(2)}) collective-permute-start(f32[64,128]{1,0:T(8,128)S(1)} %collective-permute-done.16), channel_id=1, source_target_pairs={{0,8},{1,9},{2,10},{3,11},{4,12},{5,13},{6,14},{7,15},{8,0},{9,1},... | collective-permute-start | bytes 98312 | tf_op jit(solution)/shard_map/ppermute | solution.py:199
  40.3 4.6 %collective-permute-start.15 = (f32[128,128]{1,0:T(8,128)S(1)}, f32[128,128]{1,0:T(8,128)S(1)}, u32[]{:S(2)}, u32[]{:S(2)}) collective-permute-start(f32[128,128]{1,0:T(8,128)S(1)} %join.4), channel_id=1, source_target_pairs={{0,16},{1,17},{2,18},{3,19},{4,20},{5,21},{6,22},{7,23},{8,24},{9,... | collective-permute-start | bytes 196616 | tf_op jit(solution)/shard_map/ppermute | solution.py:199
  46.2 6.7 %collective-permute-start.18 = (f32[112,128]{1,0:T(8,128)S(1)}, f32[112,128]{1,0:T(8,128)S(1)}, u32[]{:S(2)}, u32[]{:S(2)}) collective-permute-start(f32[112,128]{1,0:T(8,128)S(1)} %src_dst_part.3.refs_0_), channel_id=1, source_target_pairs={{0,1},{1,0},{2,3},{3,2},{4,5},{5,4},{6,7},{7,6},{8,9},{9,8},{10,11... | collective-permute-start | bytes 172040 | tf_op jit(solution)/shard_map/ppermute | solution.py:199
  47.1 6.5 %collective-permute-start.19 = (f32[112,128]{1,0:T(8,128)S(1)}, f32[112,128]{1,0:T(8,128)S(1)}, u32[]{:S(2)}, u32[]{:S(2)}) collective-permute-start(f32[112,128]{1,0:T(8,128)S(1)} %src_dst_part.3.refs_0_), channel_id=1, source_target_pairs={{0,2},{1,3},{2,0},{3,1},{4,6},{5,7},{6,4},{7,5},{8,10},{9,11},{10,... | collective-permute-start | bytes 172040 | tf_op jit(solution)/shard_map/ppermute | solution.py:199
  48.8 6.1 %collective-permute-start.20 = (f32[112,128]{1,0:T(8,128)S(1)}, f32[112,128]{1,0:T(8,128)S(1)}, u32[]{:S(2)}, u32[]{:S(2)}) collective-permute-start(f32[112,128]{1,0:T(8,128)S(1)} %src_dst_part.3.refs_0_), channel_id=1, source_target_pairs={{0,3},{1,2},{2,1},{3,0},{4,7},{5,6},{6,5},{7,4},{8,11},{9,10},{10,... | collective-permute-start | bytes 172040 | tf_op jit(solution)/shard_map/ppermute | solution.py:199
  51.6 1.3 %collective-permute-start.21 = (f32[64,128]{1,0:T(8,128)S(1)}, f32[64,128]{1,0:T(8,128)S(1)}, u32[]{:S(2)}, u32[]{:S(2)}) collective-permute-start(f32[64,128]{1,0:T(8,128)S(1)} %time_part.5), channel_id=1, source_target_pairs={{0,8},{1,9},{2,10},{3,11},{4,12},{5,13},{6,14},{7,15},{8,0},{9,1},... | collective-permute-start | bytes 98312 | tf_op jit(solution)/shard_map/ppermute | solution.py:199
  55.1 8.0 %collective-permute-start.22 = (f32[96,128]{1,0:T(8,128)S(1)}, f32[96,128]{1,0:T(8,128)S(1)}, u32[]{:S(2)}, u32[]{:S(2)}) collective-permute-start(f32[96,128]{1,0:T(8,128)S(1)} %get-tuple-element.23), channel_id=1, source_target_pairs={{0,4},{1,5},{2,6},{3,7},{4,0},{5,1},{6,2},{7,3},{8,12},{9,13},{10,... | collective-permute-start | bytes 147464 | tf_op jit(solution)/shard_map/ppermute | solution.py:199
  56.7 4.8 %collective-permute-start.23 = (f32[80,128]{1,0:T(8,128)S(1)}, f32[80,128]{1,0:T(8,128)S(1)}, u32[]{:S(2)}, u32[]{:S(2)}) collective-permute-start(f32[80,128]{1,0:T(8,128)S(1)} %get-tuple-element.24.own), channel_id=1, source_target_pairs={{0,8},{1,9},{2,10},{3,11},{4,12},{5,13},{6,14},{7,15},{8,0},{9,1},... | collective-permute-start | bytes 122888 | tf_op jit(solution)/shard_map/ppermute | solution.py:199
  56.7 4.8 %collective-permute-start.25 = (f32[64,128]{1,0:T(8,128)S(1)}, f32[64,128]{1,0:T(8,128)S(1)}, u32[]{:S(2)}, u32[]{:S(2)}) collective-permute-start(f32[64,128]{1,0:T(8,128)S(1)} %time_part.5), channel_id=1, source_target_pairs={{0,20},{1,21},{2,22},{3,23},{4,16},{5,17},{6,18},{7,19},{8,28},{9,... | collective-permute-start | bytes 98312 | tf_op jit(solution)/shard_map/ppermute | solution.py:199
  61.5 2.3 %collective-permute-start.26 = (f32[64,128]{1,0:T(8,128)S(1)}, f32[64,128]{1,0:T(8,128)S(1)}, u32[]{:S(2)}, u32[]{:S(2)}) collective-permute-start(f32[64,128]{1,0:T(8,128)S(1)} %collective-permute-done.25), channel_id=1, source_target_pairs={{0,8},{1,9},{2,10},{3,11},{4,12},{5,13},{6,14},{7,15},{8,0},{9,1},... | collective-permute-start | bytes 98312 | tf_op jit(solution)/shard_map/ppermute | solution.py:199
  61.5 4.6 %collective-permute-start.24 = (f32[128,128]{1,0:T(8,128)S(1)}, f32[128,128]{1,0:T(8,128)S(1)}, u32[]{:S(2)}, u32[]{:S(2)}) collective-permute-start(f32[128,128]{1,0:T(8,128)S(1)} %join.5), channel_id=1, source_target_pairs={{0,16},{1,17},{2,18},{3,19},{4,20},{5,21},{6,22},{7,23},{8,24},{9,... | collective-permute-start | bytes 196616 | tf_op jit(solution)/shard_map/ppermute | solution.py:199

commit v3 on v2

--- a/solution.py
+++ b/solution.py
@@ -33,16 +33,17 @@
 
 
 def gram(x):
-    high, low = split(x)
-    left, right = jnp.concatenate([high, high, low], 1), jnp.concatenate([high, low, high], 1)
+    high = x.astype(bf16)
+    rest = x - high.astype(f32)
+    middle = rest.astype(bf16)
+    low = (rest - middle.astype(f32)).astype(bf16)
+    left = jnp.concatenate([high, high, middle, middle, high, low], 1)
+    right = jnp.concatenate([high, middle, high, middle, low, high], 1)
     return lax.dot_general(left, right, BY_LANES, preferred_element_type=f32)
 
 
 def times(a, b):
-    (a_high, a_low), (b_high, b_low) = split(a), split(b)
-    product = jnp.dot(a_high, b_high, preferred_element_type=f32)
-    product = product + jnp.dot(a_high, b_low, preferred_element_type=f32)
-    return product + jnp.dot(a_low, b_high, preferred_element_type=f32)
+    return jnp.dot(a, b, precision=lax.Precision.HIGHEST, preferred_element_type=f32)
 
 
 def packed(x):
@@ -61,7 +62,7 @@
     return jnp.minimum(place, count - 1), place < count
 
 
-def src_dst_part(slice_rows, traffic, src_now, dst_now, time_now, time, out, ready=None):
+def src_dst_part(slice_rows, traffic, src_now, dst_now, time_now, time, out, partial, ready=None):
     rank = src_now.shape[1]
     src_rows, dst_rows, time_rows = traffic.shape
     time_gram = gram(time_now)
@@ -71,8 +72,7 @@
     dst_wide = jnp.concatenate([dst_now, dst_now], 0).T
     src_wide = jnp.concatenate([src_now, src_now], 1)
     dst_sum = jnp.zeros((dst_rows, 2 * rank), f32)
-    rows = []
-    step = 4
+    step = 8
     for first in range(0, src_rows, step):
         if ready is not None:
             ready(first)
@@ -81,8 +81,11 @@
         for i in range(step):
             part = seen[i * dst_rows : (i + 1) * dst_rows]
             dst_sum = dst_sum + part * src_wide[first + i : first + i + 1]
-            rows.append(jnp.sum(part * dst_wide, axis=0, keepdims=True))
-    src_sum = jnp.concatenate(rows, 0)
+            eights = (part * dst_wide).reshape(dst_rows // 8, 8, 2 * rank)
+            partial[(first + i) * 8 : (first + i + 1) * 8] = jnp.sum(eights, axis=0)
+    src_sum = partial[pl.ds(0, src_rows, stride=8)]
+    for i in range(1, 8):
+        src_sum = src_sum + partial[pl.ds(i, src_rows, stride=8)]
     dst_seen = (dst_sum[:, :rank] + dst_sum[:, rank:]).T
     src_part = src_model - (src_sum[:, :rank] + src_sum[:, rank:])
     dst_part = dst_model - dst_seen
@@ -94,11 +97,11 @@
     out[top + rank :] = time[pl.ds(start, slice_rows)]
 
 
-def src_dst_kernel(slice_rows, traffic, src, dst, time, out):
-    src_dst_part(slice_rows, traffic, src[...], dst[...], time[...], time, out)
-
-
-def entry_kernel(slice_rows, traffic_in, src_in, dst_in, time_in, out, traffic, src, dst, time, arrived):
+def src_dst_kernel(slice_rows, traffic, src, dst, time, out, partial):
+    src_dst_part(slice_rows, traffic, src[...], dst[...], time[...], time, out, partial)
+
+
+def entry_kernel(slice_rows, traffic_in, src_in, dst_in, time_in, out, traffic, src, dst, time, partial, arrived):
     chunks = arrived.shape[0] - 3
     chunk = traffic.shape[0] // chunks
     small = [
@@ -120,7 +123,7 @@
         if first % chunk == 0:
             large[first // chunk].wait()
 
-    src_dst_part(slice_rows, traffic, src[...], dst[...], time[...], time, out, ready)
+    src_dst_part(slice_rows, traffic, src[...], dst[...], time[...], time, out, partial, ready)
 
 
 def time_kernel(traffic, src, dst, time, out):
@@ -206,6 +209,7 @@
     dst_rows, time_rows = dst_factor.shape[0], time_factor.shape[0]
     src_top = rank * src_rows // LANES if src_rows < LANES else src_rows
     mixed_shape = jax.ShapeDtypeStruct((src_top + rank + slice_rows, LANES), f32)
+    partial_sums = pltpu.VMEM((src_rows * 8 + 8, 2 * rank), f32)
     zero_kernel = pl.pallas_call(
         functools.partial(entry_kernel, slice_rows),
         out_shape=(
@@ -217,7 +221,7 @@
         ),
         in_specs=[pl.BlockSpec(memory_space=pltpu.HBM)] * 4,
         out_specs=(VMEM,) * 5,
-        scratch_shapes=[pltpu.SemaphoreType.DMA((4 + 3,))],
+        scratch_shapes=[partial_sums, pltpu.SemaphoreType.DMA((2 + 3,))],
         compiler_params=PARAMS,
         name="entry",
     )
@@ -226,6 +230,7 @@
         out_shape=mixed_shape,
         in_specs=[VMEM] * 4,
         out_specs=VMEM,
+        scratch_shapes=[partial_sums],
         compiler_params=PARAMS,
         name="src_dst_part",
     )

time: 66.9 us -> 66.6 us (level)
  transfers between devices with their start and end apart: 27 -> 27, of which waited for: 15 -> 16; matrix products, arithmetic and copies ran while one was open for 1% -> 1% of each run, Pallas kernels for 5% -> 5%
where the time goes in v3:
time: 66.6 us; the launch traced here: 66.5 us
  starting transfers between devices  27.6 us (41%)
  waiting for transfers between devices  27.6 us (41%)
  Pallas kernels  8.9 us (13%)
  other arithmetic  1.36 us (2%)
  between operations  0.78 us (1%)
    ppermute x27, starting transfers between devices, exchanged(): return lax.ppermute(x, AXES, route)  27.6 us
    ppermute x27, waiting for transfers between devices, exchanged(): return lax.ppermute(x, AXES, route)  27.6 us
    pallas_call x3, Pallas kernels, on_device(): time_part = second_kernel(traffic, src_now, dst_now, time_now)  3.31 us
    pallas_call x2, Pallas kernels, on_device(): mixed = first_kernel(traffic, src_now, dst_now, time_now)  2.54 us
    pallas_call x1, Pallas kernels, on_device(): mixed, traffic, src_now, dst_now, time_now = zero_kernel(*given)  2.46 us
  transfers between devices with their start and end apart: 27, of which 16 were waited for; matrix products, arithmetic and copies ran while one was open for 1% of the time, Pallas kernels for 5%

profile of v3, /device:TPU:0, one launch (start us, length us, event | category | flops | bytes accessed | tf_op | source)
XLA Modules:
  0.0 66.5 jit_solution(16932235348813987335)
XLA Ops:
  0.6 2.5 %entry.1 = (f32[112,128]{1,0:T(8,128)S(1)}, bf16[64,128,128]{2,1,0:T(8,128)(2,1)S(1)}, f32[64,64]{1,0:T(8,128)S(1)}, f32[64,128]{1,0:T(8,128)S(1)}, f32[64,128]{1,0:T(8,128)S(1)}) custom-call(bf16[64,128,128]{2,1,0:T(8,128)(2,1)} %traffic_in.1, f32[64,64]{1,0:T(8,128)} %src_in.1, f32[64,128]{1,0:T(8,128)} %bitcast.6, f32[64,128]{1,0:T(8,128)} %bitcast.7), custom_call_target="tpu_custom_call" | custom-call | tf_op jit(solution)/shard_map/entry/pallas_call | solution.py:268
  3.1 3.1 %collective-permute-start = (f32[112,128]{1,0:T(8,128)S(1)}, f32[112,128]{1,0:T(8,128)S(1)}, u32[]{:S(2)}, u32[]{:S(2)}) collective-permute-start(f32[112,128]{1,0:T(8,128)S(1)} %get-tuple-element.16.refs_0_), channel_id=1, source_target_pairs={{0,1},{1,0},{2,3},{3,2},{4,5},{5,4},{6,7},{7,6},{8,9},{9,8},{10,11... | collective-permute-start | bytes 172040 | tf_op jit(solution)/shard_map/ppermute | solution.py:202
  6.2 2.6 %collective-permute-start.1 = (f32[112,128]{1,0:T(8,128)S(1)}, f32[112,128]{1,0:T(8,128)S(1)}, u32[]{:S(2)}, u32[]{:S(2)}) collective-permute-start(f32[112,128]{1,0:T(8,128)S(1)} %get-tuple-element.16.refs_0_), channel_id=1, source_target_pairs={{0,2},{1,3},{2,0},{3,1},{4,6},{5,7},{6,4},{7,5},{8,10},{9,11},{10,... | collective-permute-start | bytes 172040 | tf_op jit(solution)/shard_map/ppermute | solution.py:202
  8.8 1.1 %time_part.3 = f32[64,128]{1,0:T(8,128)S(1)} custom-call(bf16[64,128,128]{2,1,0:T(8,128)(2,1)S(1)} %get-tuple-element.14.traffic, f32[64,64]{1,0:T(8,128)S(1)} %get-tuple-element.15.src, f32[64,128]{1,0:T(8,128)S(1)} %get-tuple-element.17.dst, f32[64,128]{1,0:T(8,128)S(1)} %get-tuple-element.18.time), custom_call_target="tpu_custom_call" | custom-call | tf_op jit(solution)/shard_map/time_part/pallas_call | solution.py:274
  9.9 0.1 collective-permute-start.3
  10.0 1.2 %collective-permute-done.3 = f32[64,128]{1,0:T(8,128)S(1)} collective-permute-done((f32[64,128]{1,0:T(8,128)S(1)}, f32[64,128]{1,0:T(8,128)S(1)}, u32[]{:S(2)}, u32[]{:S(2)}) %collective-permute-start.3) | collective-permute-done | bytes 32800 | tf_op jit(solution)/shard_map/ppermute | solution.py:202
  11.2 1.2 %collective-permute-done.1.refs_2_ = f32[112,128]{1,0:T(8,128)S(1)} collective-permute-done((f32[112,128]{1,0:T(8,128)S(1)}, f32[112,128]{1,0:T(8,128)S(1)}, u32[]{:S(2)}, u32[]{:S(2)}) %collective-permute-start.1) | collective-permute-done | bytes 57376 | tf_op jit(solution)/shard_map/ppermute | solution.py:202
  12.4 2.4 %collective-permute-done.2.refs_3_ = f32[112,128]{1,0:T(8,128)S(1)} collective-permute-done((f32[112,128]{1,0:T(8,128)S(1)}, f32[112,128]{1,0:T(8,128)S(1)}, u32[]{:S(2)}, u32[]{:S(2)}) %collective-permute-start.2) | collective-permute-done | bytes 57376 | tf_op jit(solution)/shard_map/ppermute | solution.py:202
  14.8 0.2 tm_sums.3
  15.0 1.6 %collective-permute-start.4 = (f32[96,128]{1,0:T(8,128)S(1)}, f32[96,128]{1,0:T(8,128)S(1)}, u32[]{:S(2)}, u32[]{:S(2)}) collective-permute-start(f32[96,128]{1,0:T(8,128)S(1)} %get-tuple-element.19), channel_id=1, source_target_pairs={{0,4},{1,5},{2,6},{3,7},{4,0},{5,1},{6,2},{7,3},{8,12},{9,13},{10,... | collective-permute-start | bytes 147464 | tf_op jit(solution)/shard_map/ppermute | solution.py:202
  16.5 1.4 %collective-permute-start.7 = (f32[64,128]{1,0:T(8,128)S(1)}, f32[64,128]{1,0:T(8,128)S(1)}, u32[]{:S(2)}, u32[]{:S(2)}) collective-permute-start(f32[64,128]{1,0:T(8,128)S(1)} %time_part.3), channel_id=1, source_target_pairs={{0,20},{1,21},{2,22},{3,23},{4,16},{5,17},{6,18},{7,19},{8,28},{9,... | collective-permute-start | bytes 98312 | tf_op jit(solution)/shard_map/ppermute | solution.py:202
  18.0 3.4 %collective-permute-done.7 = f32[64,128]{1,0:T(8,128)S(1)} collective-permute-done((f32[64,128]{1,0:T(8,128)S(1)}, f32[64,128]{1,0:T(8,128)S(1)}, u32[]{:S(2)}, u32[]{:S(2)}) %collective-permute-start.7) | collective-permute-done | bytes 32800 | tf_op jit(solution)/shard_map/ppermute | solution.py:202
  21.4 1.6 %collective-permute-start.6 = (f32[128,128]{1,0:T(8,128)S(1)}, f32[128,128]{1,0:T(8,128)S(1)}, u32[]{:S(2)}, u32[]{:S(2)}) collective-permute-start(f32[128,128]{1,0:T(8,128)S(1)} %join.3), channel_id=1, source_target_pairs={{0,16},{1,17},{2,18},{3,19},{4,20},{5,21},{6,22},{7,23},{8,24},{9,... | collective-permute-start | bytes 196616 | tf_op jit(solution)/shard_map/ppermute | solution.py:202
  23.0 0.1 fusion.19
  23.1 2.9 %collective-permute-done.6 = f32[128,128]{1,0:T(8,128)S(1)} collective-permute-done((f32[128,128]{1,0:T(8,128)S(1)}, f32[128,128]{1,0:T(8,128)S(1)}, u32[]{:S(2)}, u32[]{:S(2)}) %collective-permute-start.6) | collective-permute-done | bytes 65568 | tf_op jit(solution)/shard_map/ppermute | solution.py:202
  26.0 1.3 %src_dst_part.2.refs_0_ = f32[112,128]{1,0:T(8,128)S(1)} custom-call(bf16[64,128,128]{2,1,0:T(8,128)(2,1)S(1)} %get-tuple-element.14.traffic, f32[64,64]{1,0:T(8,128)S(1)} %fusion.15.src, f32[64,128]{1,0:T(8,128)S(1)} %get-tuple-element.30.dst, f32[64,128]{1,0:T(8,128)S(1)} %get-tuple-element.29.time), custom_call_target="tpu_custom_call" | custom-call | tf_op jit(solution)/shard_map/src_dst_part/pallas_call | solution.py:270
  27.3 1.0 %collective-permute-start.10 = (f32[112,128]{1,0:T(8,128)S(1)}, f32[112,128]{1,0:T(8,128)S(1)}, u32[]{:S(2)}, u32[]{:S(2)}) collective-permute-start(f32[112,128]{1,0:T(8,128)S(1)} %src_dst_part.2.refs_0_), channel_id=1, source_target_pairs={{0,2},{1,3},{2,0},{3,1},{4,6},{5,7},{6,4},{7,5},{8,10},{9,11},{10,... | collective-permute-start | bytes 172040 | tf_op jit(solution)/shard_map/ppermute | solution.py:202
  28.3 0.8 %collective-permute-start.11 = (f32[112,128]{1,0:T(8,128)S(1)}, f32[112,128]{1,0:T(8,128)S(1)}, u32[]{:S(2)}, u32[]{:S(2)}) collective-permute-start(f32[112,128]{1,0:T(8,128)S(1)} %src_dst_part.2.refs_0_), channel_id=1, source_target_pairs={{0,3},{1,2},{2,1},{3,0},{4,7},{5,6},{6,5},{7,4},{8,11},{9,10},{10,... | collective-permute-start | bytes 172040 | tf_op jit(solution)/shard_map/ppermute | solution.py:202
  29.1 1.7 %collective-permute-start.9 = (f32[112,128]{1,0:T(8,128)S(1)}, f32[112,128]{1,0:T(8,128)S(1)}, u32[]{:S(2)}, u32[]{:S(2)}) collective-permute-start(f32[112,128]{1,0:T(8,128)S(1)} %src_dst_part.2.refs_0_), channel_id=1, source_target_pairs={{0,1},{1,0},{2,3},{3,2},{4,5},{5,4},{6,7},{7,6},{8,9},{9,8},{10,11... | collective-permute-start | bytes 172040 | tf_op jit(solution)/shard_map/ppermute | solution.py:202
  30.8 1.1 %time_part.4 = f32[64,128]{1,0:T(8,128)S(1)} custom-call(bf16[64,128,128]{2,1,0:T(8,128)(2,1)S(1)} %get-tuple-element.14.traffic, f32[64,64]{1,0:T(8,128)S(1)} %fusion.15.src, f32[64,128]{1,0:T(8,128)S(1)} %get-tuple-element.30.dst, f32[64,128]{1,0:T(8,128)S(1)} %get-tuple-element.29.time), custom_call_target="tpu_custom_call" | custom-call | tf_op jit(solution)/shard_map/time_part/pallas_call | solution.py:274
  31.9 0.1 collective-permute-start.12
  32.0 1.2 %collective-permute-done.12 = f32[64,128]{1,0:T(8,128)S(1)} collective-permute-done((f32[64,128]{1,0:T(8,128)S(1)}, f32[64,128]{1,0:T(8,128)S(1)}, u32[]{:S(2)}, u32[]{:S(2)}) %collective-permute-start.12) | collective-permute-done | bytes 32800 | tf_op jit(solution)/shard_map/ppermute | solution.py:202
  33.2 0.3 collective-permute-done.10.refs_2_
  33.5 0.8 %collective-permute-done.11.refs_3_ = f32[112,128]{1,0:T(8,128)S(1)} collective-permute-done((f32[112,128]{1,0:T(8,128)S(1)}, f32[112,128]{1,0:T(8,128)S(1)}, u32[]{:S(2)}, u32[]{:S(2)}) %collective-permute-start.11) | collective-permute-done | bytes 57376 | tf_op jit(solution)/shard_map/ppermute | solution.py:202
  34.4 0.2 tm_sums.4
  34.6 0.6 collective-permute-start.13
  35.2 2.4 %collective-permute-start.16 = (f32[64,128]{1,0:T(8,128)S(1)}, f32[64,128]{1,0:T(8,128)S(1)}, u32[]{:S(2)}, u32[]{:S(2)}) collective-permute-start(f32[64,128]{1,0:T(8,128)S(1)} %time_part.4), channel_id=1, source_target_pairs={{0,20},{1,21},{2,22},{3,23},{4,16},{5,17},{6,18},{7,19},{8,28},{9,... | collective-permute-start | bytes 98312 | tf_op jit(solution)/shard_map/ppermute | solution.py:202
  37.6 2.4 %collective-permute-done.16 = f32[64,128]{1,0:T(8,128)S(1)} collective-permute-done((f32[64,128]{1,0:T(8,128)S(1)}, f32[64,128]{1,0:T(8,128)S(1)}, u32[]{:S(2)}, u32[]{:S(2)}) %collective-permute-start.16) | collective-permute-done | bytes 32800 | tf_op jit(solution)/shard_map/ppermute | solution.py:202
  40.0 1.5 %collective-permute-start.15 = (f32[128,128]{1,0:T(8,128)S(1)}, f32[128,128]{1,0:T(8,128)S(1)}, u32[]{:S(2)}, u32[]{:S(2)}) collective-permute-start(f32[128,128]{1,0:T(8,128)S(1)} %join.4), channel_id=1, source_target_pairs={{0,16},{1,17},{2,18},{3,19},{4,20},{5,21},{6,22},{7,23},{8,24},{9,... | collective-permute-start | bytes 196616 | tf_op jit(solution)/shard_map/ppermute | solution.py:202
  41.6 0.1 fusion.18
  41.7 2.9 %collective-permute-done.15 = f32[128,128]{1,0:T(8,128)S(1)} collective-permute-done((f32[128,128]{1,0:T(8,128)S(1)}, f32[128,128]{1,0:T(8,128)S(1)}, u32[]{:S(2)}, u32[]{:S(2)}) %collective-permute-start.15) | collective-permute-done | bytes 65568 | tf_op jit(solution)/shard_map/ppermute | solution.py:202
  44.6 1.3 %src_dst_part.3.refs_0_ = f32[112,128]{1,0:T(8,128)S(1)} custom-call(bf16[64,128,128]{2,1,0:T(8,128)(2,1)S(1)} %get-tuple-element.14.traffic, f32[64,64]{1,0:T(8,128)S(1)} %fusion.16.src, f32[64,128]{1,0:T(8,128)S(1)} %get-tuple-element.28.dst, f32[64,128]{1,0:T(8,128)S(1)} %get-tuple-element.27.time), custom_call_target="tpu_custom_call" | custom-call | tf_op jit(solution)/shard_map/src_dst_part/pallas_call | solution.py:270
  45.9 1.0 %collective-permute-start.18 = (f32[112,128]{1,0:T(8,128)S(1)}, f32[112,128]{1,0:T(8,128)S(1)}, u32[]{:S(2)}, u32[]{:S(2)}) collective-permute-start(f32[112,128]{1,0:T(8,128)S(1)} %src_dst_part.3.refs_0_), channel_id=1, source_target_pairs={{0,1},{1,0},{2,3},{3,2},{4,5},{5,4},{6,7},{7,6},{8,9},{9,8},{10,11... | collective-permute-start | bytes 172040 | tf_op jit(solution)/shard_map/ppermute | solution.py:202
  46.9 1.7 %collective-permute-start.19 = (f32[112,128]{1,0:T(8,128)S(1)}, f32[112,128]{1,0:T(8,128)S(1)}, u32[]{:S(2)}, u32[]{:S(2)}) collective-permute-start(f32[112,128]{1,0:T(8,128)S(1)} %src_dst_part.3.refs_0_), channel_id=1, source_target_pairs={{0,2},{1,3},{2,0},{3,1},{4,6},{5,7},{6,4},{7,5},{8,10},{9,11},{10,... | collective-permute-start | bytes 172040 | tf_op jit(solution)/shard_map/ppermute | solution.py:202
  48.6 1.8 %collective-permute-start.20 = (f32[112,128]{1,0:T(8,128)S(1)}, f32[112,128]{1,0:T(8,128)S(1)}, u32[]{:S(2)}, u32[]{:S(2)}) collective-permute-start(f32[112,128]{1,0:T(8,128)S(1)} %src_dst_part.3.refs_0_), channel_id=1, source_target_pairs={{0,3},{1,2},{2,1},{3,0},{4,7},{5,6},{6,5},{7,4},{8,11},{9,10},{10,... | collective-permute-start | bytes 172040 | tf_op jit(solution)/shard_map/ppermute | solution.py:202
  50.3 1.1 %time_part.5 = f32[64,128]{1,0:T(8,128)S(1)} custom-call(bf16[64,128,128]{2,1,0:T(8,128)(2,1)S(1)} %get-tuple-element.14.traffic, f32[64,64]{1,0:T(8,128)S(1)} %fusion.16.src, f32[64,128]{1,0:T(8,128)S(1)} %get-tuple-element.28.dst, f32[64,128]{1,0:T(8,128)S(1)} %get-tuple-element.27.time), custom_call_target="tpu_custom_call" | custom-call | tf_op jit(solution)/shard_map/time_part/pallas_call | solution.py:274
  51.5 1.2 %collective-permute-done.21 = f32[64,128]{1,0:T(8,128)S(1)} collective-permute-done((f32[64,128]{1,0:T(8,128)S(1)}, f32[64,128]{1,0:T(8,128)S(1)}, u32[]{:S(2)}, u32[]{:S(2)}) %collective-permute-start.21) | collective-permute-done | bytes 32800 | tf_op jit(solution)/shard_map/ppermute | solution.py:202
  52.7 0.7 %collective-permute-done.19.refs_2_ = f32[112,128]{1,0:T(8,128)S(1)} collective-permute-done((f32[112,128]{1,0:T(8,128)S(1)}, f32[112,128]{1,0:T(8,128)S(1)}, u32[]{:S(2)}, u32[]{:S(2)}) %collective-permute-start.19) | collective-permute-done | bytes 57376 | tf_op jit(solution)/shard_map/ppermute | solution.py:202
  53.4 1.2 %collective-permute-done.20.refs_3_ = f32[112,128]{1,0:T(8,128)S(1)} collective-permute-done((f32[112,128]{1,0:T(8,128)S(1)}, f32[112,128]{1,0:T(8,128)S(1)}, u32[]{:S(2)}, u32[]{:S(2)}) %collective-permute-start.20) | collective-permute-done | bytes 57376 | tf_op jit(solution)/shard_map/ppermute | solution.py:202
  54.6 0.2 tm_sums.5
  54.8 1.6 %collective-permute-start.22 = (f32[96,128]{1,0:T(8,128)S(1)}, f32[96,128]{1,0:T(8,128)S(1)}, u32[]{:S(2)}, u32[]{:S(2)}) collective-permute-start(f32[96,128]{1,0:T(8,128)S(1)} %get-tuple-element.23), channel_id=1, source_target_pairs={{0,4},{1,5},{2,6},{3,7},{4,0},{5,1},{6,2},{7,3},{8,12},{9,13},{10,... | collective-permute-start | bytes 147464 | tf_op jit(solution)/shard_map/ppermute | solution.py:202
  56.4 1.4 %collective-permute-start.25 = (f32[64,128]{1,0:T(8,128)S(1)}, f32[64,128]{1,0:T(8,128)S(1)}, u32[]{:S(2)}, u32[]{:S(2)}) collective-permute-start(f32[64,128]{1,0:T(8,128)S(1)} %time_part.5), channel_id=1, source_target_pairs={{0,20},{1,21},{2,22},{3,23},{4,16},{5,17},{6,18},{7,19},{8,28},{9,... | collective-permute-start | bytes 98312 | tf_op jit(solution)/shard_map/ppermute | solution.py:202
  57.8 3.4 %collective-permute-done.25 = f32[64,128]{1,0:T(8,128)S(1)} collective-permute-done((f32[64,128]{1,0:T(8,128)S(1)}, f32[64,128]{1,0:T(8,128)S(1)}, u32[]{:S(2)}, u32[]{:S(2)}) %collective-permute-start.25) | collective-permute-done | bytes 32800 | tf_op jit(solution)/shard_map/ppermute | solution.py:202
  61.2 1.6 %collective-permute-start.24 = (f32[128,128]{1,0:T(8,128)S(1)}, f32[128,128]{1,0:T(8,128)S(1)}, u32[]{:S(2)}, u32[]{:S(2)}) collective-permute-start(f32[128,128]{1,0:T(8,128)S(1)} %join.5), channel_id=1, source_target_pairs={{0,16},{1,17},{2,18},{3,19},{4,20},{5,21},{6,22},{7,23},{8,24},{9,... | collective-permute-start | bytes 196616 | tf_op jit(solution)/shard_map/ppermute | solution.py:202
  62.8 0.1 fusion.17
  62.9 0.6 maximum_multiply_fusion.2
  63.5 2.3 %collective-permute-done.24 = f32[128,128]{1,0:T(8,128)S(1)} collective-permute-done((f32[128,128]{1,0:T(8,128)S(1)}, f32[128,128]{1,0:T(8,128)S(1)}, u32[]{:S(2)}, u32[]{:S(2)}) %collective-permute-start.24) | collective-permute-done | bytes 65568 | tf_op jit(solution)/shard_map/ppermute | solution.py:202
  65.8 0.6 fusion.2
  (33 shorter events, 0.3 us)
Async XLA Ops:
  3.1 8.1 %collective-permute-start = (f32[112,128]{1,0:T(8,128)S(1)}, f32[112,128]{1,0:T(8,128)S(1)}, u32[]{:S(2)}, u32[]{:S(2)}) collective-permute-start(f32[112,128]{1,0:T(8,128)S(1)} %get-tuple-element.16.refs_0_), channel_id=1, source_target_pairs={{0,1},{1,0},{2,3},{3,2},{4,5},{5,4},{6,7},{7,6},{8,9},{9,8},{10,11... | collective-permute-start | bytes 172040 | tf_op jit(solution)/shard_map/ppermute | solution.py:202
  6.2 6.2 %collective-permute-start.1 = (f32[112,128]{1,0:T(8,128)S(1)}, f32[112,128]{1,0:T(8,128)S(1)}, u32[]{:S(2)}, u32[]{:S(2)}) collective-permute-start(f32[112,128]{1,0:T(8,128)S(1)} %get-tuple-element.16.refs_0_), channel_id=1, source_target_pairs={{0,2},{1,3},{2,0},{3,1},{4,6},{5,7},{6,4},{7,5},{8,10},{9,11},{10,... | collective-permute-start | bytes 172040 | tf_op jit(solution)/shard_map/ppermute | solution.py:202
  8.8 6.0 %collective-permute-start.2 = (f32[112,128]{1,0:T(8,128)S(1)}, f32[112,128]{1,0:T(8,128)S(1)}, u32[]{:S(2)}, u32[]{:S(2)}) collective-permute-start(f32[112,128]{1,0:T(8,128)S(1)} %get-tuple-element.16.refs_0_), channel_id=1, source_target_pairs={{0,3},{1,2},{2,1},{3,0},{4,7},{5,6},{6,5},{7,4},{8,11},{9,10},{10,... | collective-permute-start | bytes 172040 | tf_op jit(solution)/shard_map/ppermute | solution.py:202
  9.9 1.3 %collective-permute-start.3 = (f32[64,128]{1,0:T(8,128)S(1)}, f32[64,128]{1,0:T(8,128)S(1)}, u32[]{:S(2)}, u32[]{:S(2)}) collective-permute-start(f32[64,128]{1,0:T(8,128)S(1)} %time_part.3), channel_id=1, source_target_pairs={{0,8},{1,9},{2,10},{3,11},{4,12},{5,13},{6,14},{7,15},{8,0},{9,1},... | collective-permute-start | bytes 98312 | tf_op jit(solution)/shard_map/ppermute | solution.py:202
  15.0 8.0 %collective-permute-start.4 = (f32[96,128]{1,0:T(8,128)S(1)}, f32[96,128]{1,0:T(8,128)S(1)}, u32[]{:S(2)}, u32[]{:S(2)}) collective-permute-start(f32[96,128]{1,0:T(8,128)S(1)} %get-tuple-element.19), channel_id=1, source_target_pairs={{0,4},{1,5},{2,6},{3,7},{4,0},{5,1},{6,2},{7,3},{8,12},{9,13},{10,... | collective-permute-start | bytes 147464 | tf_op jit(solution)/shard_map/ppermute | solution.py:202
  16.5 4.8 %collective-permute-start.5 = (f32[80,128]{1,0:T(8,128)S(1)}, f32[80,128]{1,0:T(8,128)S(1)}, u32[]{:S(2)}, u32[]{:S(2)}) collective-permute-start(f32[80,128]{1,0:T(8,128)S(1)} %get-tuple-element.20.own), channel_id=1, source_target_pairs={{0,8},{1,9},{2,10},{3,11},{4,12},{5,13},{6,14},{7,15},{8,0},{9,1},... | collective-permute-start | bytes 122888 | tf_op jit(solution)/shard_map/ppermute | solution.py:202
  16.5 4.8 %collective-permute-start.7 = (f32[64,128]{1,0:T(8,128)S(1)}, f32[64,128]{1,0:T(8,128)S(1)}, u32[]{:S(2)}, u32[]{:S(2)}) collective-permute-start(f32[64,128]{1,0:T(8,128)S(1)} %time_part.3), channel_id=1, source_target_pairs={{0,20},{1,21},{2,22},{3,23},{4,16},{5,17},{6,18},{7,19},{8,28},{9,... | collective-permute-start | bytes 98312 | tf_op jit(solution)/shard_map/ppermute | solution.py:202
  21.4 1.7 %collective-permute-start.8 = (f32[64,128]{1,0:T(8,128)S(1)}, f32[64,128]{1,0:T(8,128)S(1)}, u32[]{:S(2)}, u32[]{:S(2)}) collective-permute-start(f32[64,128]{1,0:T(8,128)S(1)} %collective-permute-done.7), channel_id=1, source_target_pairs={{0,8},{1,9},{2,10},{3,11},{4,12},{5,13},{6,14},{7,15},{8,0},{9,1},... | collective-permute-start | bytes 98312 | tf_op jit(solution)/shard_map/ppermute | solution.py:202
  21.4 4.6 %collective-permute-start.6 = (f32[128,128]{1,0:T(8,128)S(1)}, f32[128,128]{1,0:T(8,128)S(1)}, u32[]{:S(2)}, u32[]{:S(2)}) collective-permute-start(f32[128,128]{1,0:T(8,128)S(1)} %join.3), channel_id=1, source_target_pairs={{0,16},{1,17},{2,18},{3,19},{4,20},{5,21},{6,22},{7,23},{8,24},{9,... | collective-permute-start | bytes 196616 | tf_op jit(solution)/shard_map/ppermute | solution.py:202
  27.3 6.3 %collective-permute-start.10 = (f32[112,128]{1,0:T(8,128)S(1)}, f32[112,128]{1,0:T(8,128)S(1)}, u32[]{:S(2)}, u32[]{:S(2)}) collective-permute-start(f32[112,128]{1,0:T(8,128)S(1)} %src_dst_part.2.refs_0_), channel_id=1, source_target_pairs={{0,2},{1,3},{2,0},{3,1},{4,6},{5,7},{6,4},{7,5},{8,10},{9,11},{10,... | collective-permute-start | bytes 172040 | tf_op jit(solution)/shard_map/ppermute | solution.py:202
  28.3 6.1 %collective-permute-start.11 = (f32[112,128]{1,0:T(8,128)S(1)}, f32[112,128]{1,0:T(8,128)S(1)}, u32[]{:S(2)}, u32[]{:S(2)}) collective-permute-start(f32[112,128]{1,0:T(8,128)S(1)} %src_dst_part.2.refs_0_), channel_id=1, source_target_pairs={{0,3},{1,2},{2,1},{3,0},{4,7},{5,6},{6,5},{7,4},{8,11},{9,10},{10,... | collective-permute-start | bytes 172040 | tf_op jit(solution)/shard_map/ppermute | solution.py:202
  29.1 5.3 %collective-permute-start.9 = (f32[112,128]{1,0:T(8,128)S(1)}, f32[112,128]{1,0:T(8,128)S(1)}, u32[]{:S(2)}, u32[]{:S(2)}) collective-permute-start(f32[112,128]{1,0:T(8,128)S(1)} %src_dst_part.2.refs_0_), channel_id=1, source_target_pairs={{0,1},{1,0},{2,3},{3,2},{4,5},{5,4},{6,7},{7,6},{8,9},{9,8},{10,11... | collective-permute-start | bytes 172040 | tf_op jit(solution)/shard_map/ppermute | solution.py:202
  31.9 1.3 %collective-permute-start.12 = (f32[64,128]{1,0:T(8,128)S(1)}, f32[64,128]{1,0:T(8,128)S(1)}, u32[]{:S(2)}, u32[]{:S(2)}) collective-permute-start(f32[64,128]{1,0:T(8,128)S(1)} %time_part.4), channel_id=1, source_target_pairs={{0,8},{1,9},{2,10},{3,11},{4,12},{5,13},{6,14},{7,15},{8,0},{9,1},... | collective-permute-start | bytes 98312 | tf_op jit(solution)/shard_map/ppermute | solution.py:202
  34.6 7.0 %collective-permute-start.13 = (f32[96,128]{1,0:T(8,128)S(1)}, f32[96,128]{1,0:T(8,128)S(1)}, u32[]{:S(2)}, u32[]{:S(2)}) collective-permute-start(f32[96,128]{1,0:T(8,128)S(1)} %get-tuple-element.21), channel_id=1, source_target_pairs={{0,4},{1,5},{2,6},{3,7},{4,0},{5,1},{6,2},{7,3},{8,12},{9,13},{10,... | collective-permute-start | bytes 147464 | tf_op jit(solution)/shard_map/ppermute | solution.py:202
  35.2 4.8 %collective-permute-start.14 = (f32[80,128]{1,0:T(8,128)S(1)}, f32[80,128]{1,0:T(8,128)S(1)}, u32[]{:S(2)}, u32[]{:S(2)}) collective-permute-start(f32[80,128]{1,0:T(8,128)S(1)} %get-tuple-element.22.own), channel_id=1, source_target_pairs={{0,8},{1,9},{2,10},{3,11},{4,12},{5,13},{6,14},{7,15},{8,0},{9,1},... | collective-permute-start | bytes 122888 | tf_op jit(solution)/shard_map/ppermute | solution.py:202
  35.2 4.8 %collective-permute-start.16 = (f32[64,128]{1,0:T(8,128)S(1)}, f32[64,128]{1,0:T(8,128)S(1)}, u32[]{:S(2)}, u32[]{:S(2)}) collective-permute-start(f32[64,128]{1,0:T(8,128)S(1)} %time_part.4), channel_id=1, source_target_pairs={{0,20},{1,21},{2,22},{3,23},{4,16},{5,17},{6,18},{7,19},{8,28},{9,... | collective-permute-start | bytes 98312 | tf_op jit(solution)/shard_map/ppermute | solution.py:202
  40.0 1.7 %collective-permute-start.17 = (f32[64,128]{1,0:T(8,128)S(1)}, f32[64,128]{1,0:T(8,128)S(1)}, u32[]{:S(2)}, u32[]{:S(2)}) collective-permute-start(f32[64,128]{1,0:T(8,128)S(1)} %collective-permute-done.16), channel_id=1, source_target_pairs={{0,8},{1,9},{2,10},{3,11},{4,12},{5,13},{6,14},{7,15},{8,0},{9,1},... | collective-permute-start | bytes 98312 | tf_op jit(solution)/shard_map/ppermute | solution.py:202
  40.0 4.6 %collective-permute-start.15 = (f32[128,128]{1,0:T(8,128)S(1)}, f32[128,128]{1,0:T(8,128)S(1)}, u32[]{:S(2)}, u32[]{:S(2)}) collective-permute-start(f32[128,128]{1,0:T(8,128)S(1)} %join.4), channel_id=1, source_target_pairs={{0,16},{1,17},{2,18},{3,19},{4,20},{5,21},{6,22},{7,23},{8,24},{9,... | collective-permute-start | bytes 196616 | tf_op jit(solution)/shard_map/ppermute | solution.py:202
  45.9 6.8 %collective-permute-start.18 = (f32[112,128]{1,0:T(8,128)S(1)}, f32[112,128]{1,0:T(8,128)S(1)}, u32[]{:S(2)}, u32[]{:S(2)}) collective-permute-start(f32[112,128]{1,0:T(8,128)S(1)} %src_dst_part.3.refs_0_), channel_id=1, source_target_pairs={{0,1},{1,0},{2,3},{3,2},{4,5},{5,4},{6,7},{7,6},{8,9},{9,8},{10,11... | collective-permute-start | bytes 172040 | tf_op jit(solution)/shard_map/ppermute | solution.py:202
  46.9 6.6 %collective-permute-start.19 = (f32[112,128]{1,0:T(8,128)S(1)}, f32[112,128]{1,0:T(8,128)S(1)}, u32[]{:S(2)}, u32[]{:S(2)}) collective-permute-start(f32[112,128]{1,0:T(8,128)S(1)} %src_dst_part.3.refs_0_), channel_id=1, source_target_pairs={{0,2},{1,3},{2,0},{3,1},{4,6},{5,7},{6,4},{7,5},{8,10},{9,11},{10,... | collective-permute-start | bytes 172040 | tf_op jit(solution)/shard_map/ppermute | solution.py:202
  48.6 6.1 %collective-permute-start.20 = (f32[112,128]{1,0:T(8,128)S(1)}, f32[112,128]{1,0:T(8,128)S(1)}, u32[]{:S(2)}, u32[]{:S(2)}) collective-permute-start(f32[112,128]{1,0:T(8,128)S(1)} %src_dst_part.3.refs_0_), channel_id=1, source_target_pairs={{0,3},{1,2},{2,1},{3,0},{4,7},{5,6},{6,5},{7,4},{8,11},{9,10},{10,... | collective-permute-start | bytes 172040 | tf_op jit(solution)/shard_map/ppermute | solution.py:202
  51.5 1.3 %collective-permute-start.21 = (f32[64,128]{1,0:T(8,128)S(1)}, f32[64,128]{1,0:T(8,128)S(1)}, u32[]{:S(2)}, u32[]{:S(2)}) collective-permute-start(f32[64,128]{1,0:T(8,128)S(1)} %time_part.5), channel_id=1, source_target_pairs={{0,8},{1,9},{2,10},{3,11},{4,12},{5,13},{6,14},{7,15},{8,0},{9,1},... | collective-permute-start | bytes 98312 | tf_op jit(solution)/shard_map/ppermute | solution.py:202
  54.8 8.0 %collective-permute-start.22 = (f32[96,128]{1,0:T(8,128)S(1)}, f32[96,128]{1,0:T(8,128)S(1)}, u32[]{:S(2)}, u32[]{:S(2)}) collective-permute-start(f32[96,128]{1,0:T(8,128)S(1)} %get-tuple-element.23), channel_id=1, source_target_pairs={{0,4},{1,5},{2,6},{3,7},{4,0},{5,1},{6,2},{7,3},{8,12},{9,13},{10,... | collective-permute-start | bytes 147464 | tf_op jit(solution)/shard_map/ppermute | solution.py:202
  56.4 4.8 %collective-permute-start.23 = (f32[80,128]{1,0:T(8,128)S(1)}, f32[80,128]{1,0:T(8,128)S(1)}, u32[]{:S(2)}, u32[]{:S(2)}) collective-permute-start(f32[80,128]{1,0:T(8,128)S(1)} %get-tuple-element.24.own), channel_id=1, source_target_pairs={{0,8},{1,9},{2,10},{3,11},{4,12},{5,13},{6,14},{7,15},{8,0},{9,1},... | collective-permute-start | bytes 122888 | tf_op jit(solution)/shard_map/ppermute | solution.py:202
  56.4 4.8 %collective-permute-start.25 = (f32[64,128]{1,0:T(8,128)S(1)}, f32[64,128]{1,0:T(8,128)S(1)}, u32[]{:S(2)}, u32[]{:S(2)}) collective-permute-start(f32[64,128]{1,0:T(8,128)S(1)} %time_part.5), channel_id=1, source_target_pairs={{0,20},{1,21},{2,22},{3,23},{4,16},{5,17},{6,18},{7,19},{8,28},{9,... | collective-permute-start | bytes 98312 | tf_op jit(solution)/shard_map/ppermute | solution.py:202
  61.2 2.3 %collective-permute-start.26 = (f32[64,128]{1,0:T(8,128)S(1)}, f32[64,128]{1,0:T(8,128)S(1)}, u32[]{:S(2)}, u32[]{:S(2)}) collective-permute-start(f32[64,128]{1,0:T(8,128)S(1)} %collective-permute-done.25), channel_id=1, source_target_pairs={{0,8},{1,9},{2,10},{3,11},{4,12},{5,13},{6,14},{7,15},{8,0},{9,1},... | collective-permute-start | bytes 98312 | tf_op jit(solution)/shard_map/ppermute | solution.py:202
  61.2 4.6 %collective-permute-start.24 = (f32[128,128]{1,0:T(8,128)S(1)}, f32[128,128]{1,0:T(8,128)S(1)}, u32[]{:S(2)}, u32[]{:S(2)}) collective-permute-start(f32[128,128]{1,0:T(8,128)S(1)} %join.5), channel_id=1, source_target_pairs={{0,16},{1,17},{2,18},{3,19},{4,20},{5,21},{6,22},{7,23},{8,24},{9,... | collective-permute-start | bytes 196616 | tf_op jit(solution)/shard_map/ppermute | solution.py:202
